TPU v7x, 32 devices: a whole 2x2x4 slice. The times are simulated.
32 devices in a mesh: gx: 8 (over z, x), gy: 4 (over y, core).
Axes of the slice: x: 2, y: 2, z: 4, core: 2. Of those that a mesh axis runs over, the one named last changes fastest.
Arguments:
- reference_scan: bfloat16 [128, 128, 2048], P('gx', 'gy'), may hold values from -6 to 6
- ref_gradient: bfloat16 [3, 128, 128, 2048], P(None, 'gx', 'gy'), may hold values from -6 to 6
- deformed_scan: bfloat16 [128, 128, 2048], P('gx', 'gy'), may hold values from -6 to 6
- interp_weights: bfloat16 [128, 128, 2048], P('gx', 'gy'), may hold values from 0 to 1
- sample_mask: int32 [128, 128, 2048], P('gx', 'gy'), may hold values from 0 to 1, as said below
- block_list: int32 [8, 16384], P('gx', 'gy'), may hold values from -1 to 8191, as said below
- offsets: int32 [2, 128, 128, 4], P(None, 'gx', 'gy'), may hold values from -4 to 4, as said below
Outputs:
- increment: float32 [3, 128, 128, 5], P(None, 'gx', 'gy')
- cg_residual: float32 [3, 128, 128, 5], P(None, 'gx', 'gy')
Inputs may be any that keep to these rules, and one draw needn't show every extreme that they name: sample_mask is 0 in every block of 128 voxels that its device's block_list does not name. `block_list`: each device's 4096 entries are first distinct local block indices, then -1 to the end; some device names exactly 4096 blocks. `offsets`: both ends of the range occur.
All inputs are finite; a program needn't handle non-finite values.
Results may differ from a plain program's by a relative error of at most 0.0045.
Values may be sent and summed in bfloat16 or wider, within the bound.
A program may use at most 320 MiB of HBM per device.

v0:
```python
import functools

import jax
import jax.numpy as jnp
from jax import lax
from jax.experimental import pallas as pl
from jax.experimental.pallas import tpu as pltpu
from jax.sharding import PartitionSpec as P

BOUND = 4
ITERS = 3

tikhonov = 8.0

NODES = [(n >> 2 & 1, n >> 1 & 1, n & 1) for n in range(8)]
PAIRS = [(c, d) for c in range(3) for d in range(c, 3)]
PAIR_OF = {(c, d): PAIRS.index((min(c, d), max(c, d))) for c in range(3) for d in range(3)}
MESH = pl.DeviceIdType.MESH


def split3(table):
    first = table.astype(jnp.bfloat16)
    rest = table - first.astype(jnp.float32)
    second = rest.astype(jnp.bfloat16)
    third = (rest - second.astype(jnp.float32)).astype(jnp.bfloat16)
    return [first, second, third]


def tables():
    voxel = jnp.arange(512)
    coords = [
        ((voxel // 64).astype(jnp.float32) + 0.5) / 8.0,
        ((voxel // 8 % 8).astype(jnp.float32) + 0.5) / 8.0,
        ((voxel % 8).astype(jnp.float32) + 0.5) / 8.0,
    ]
    linear = [[1.0 - t, t] for t in coords]
    quad = [[s[0] * s[0], s[0] * s[1], s[1] * s[1]] for s in linear]
    shapes = jnp.stack([linear[0][i] * linear[1][j] * linear[2][l] for i, j, l in NODES])
    squares = jnp.stack(
        [quad[0][a] * quad[1][b] * quad[2][c] for a in range(3) for b in range(3) for c in range(3)]
    )
    squares = jnp.pad(squares, ((0, 5), (0, 0)))
    square_table = jnp.concatenate(split3(squares), axis=0)
    shape_table = jnp.concatenate(split3(shapes) + [jnp.zeros((8, 512), jnp.bfloat16)], axis=0)
    return (square_table, shape_table)


def put_split(value, high_ref, low_ref, rows, lanes):
    high = value.astype(jnp.bfloat16)
    high_ref[rows, lanes] = high
    low_ref[rows, lanes] = (value - high.astype(jnp.float32)).astype(jnp.bfloat16)


def contract(table, part):
    return lax.dot_general(
        table, part, (((1,), (1,)), ((), ())), preferred_element_type=jnp.float32
    )


def hessian_kernel(
    depth,
    sizes,
    table_ref,
    grad_ref,
    mask_ref,
    scan_ref,
    out_ref,
    before_ref,
    after_ref,
    beyond_ref,
    ahead_ref,
    high_ref,
    low_ref,
    send_sems,
    recv_sems,
):
    step = pl.program_id(0)
    tile_y = mask_ref.shape[1]
    tile_x = scan_ref.shape[0]
    gx = lax.axis_index("gx")
    gy = lax.axis_index("gy")
    not_first_x, not_last_x = (gx > 0, gx < sizes[0] - 1)
    not_first_y, not_last_y = (gy > 0, gy < sizes[1] - 1)
    both = jnp.logical_and

    def copy(k, source, target, device):
        return pltpu.make_async_remote_copy(
            src_ref=source,
            dst_ref=target,
            send_sem=send_sems.at[k],
            recv_sem=recv_sems.at[k],
            device_id=device,
            device_id_type=MESH,
        )

    every, low_y, high_y = (slice(None), pl.ds(0, 8), pl.ds(tile_y - 8, 8))
    own = pl.ds(BOUND, tile_x)
    front, back = (pl.ds(0, BOUND), pl.ds(BOUND + tile_x, BOUND + 1))
    near_y, far_y = ((gx, gy - 1), (gx, gy + 1))
    direct = [
        (
            copy(0, scan_ref.at[pl.ds(tile_x - BOUND, BOUND)], before_ref, (gx + 1, gy)),
            not_last_x,
            not_first_x,
        ),
        (
            copy(1, scan_ref.at[pl.ds(0, BOUND + 1)], after_ref, (gx - 1, gy)),
            not_first_x,
            not_last_x,
        ),
        (
            copy(2, scan_ref.at[every, low_y], beyond_ref.at[own], near_y),
            not_first_y,
            not_last_y,
        ),
        (
            copy(3, scan_ref.at[every, high_y], ahead_ref.at[own], far_y),
            not_last_y,
            not_first_y,
        ),
    ]
    forwarded = []
    for k, band, rows, present in (
        (4, before_ref, front, not_first_x),
        (6, after_ref, back, not_last_x),
    ):
        forwarded.append(
            (
                copy(k, band.at[every, low_y], beyond_ref.at[rows], near_y),
                both(present, not_first_y),
                both(present, not_last_y),
            )
        )
        forwarded.append(
            (
                copy(k + 1, band.at[every, high_y], ahead_ref.at[rows], far_y),
                both(present, not_last_y),
                both(present, not_first_y),
            )
        )

    @pl.when(step == 0)
    def _():
        barrier = pltpu.get_barrier_semaphore()
        peers = 0
        for present, device in (
            (not_first_x, (gx - 1, gy)),
            (not_last_x, (gx + 1, gy)),
            (not_first_y, near_y),
            (not_last_y, far_y),
        ):
            peers = peers + jnp.where(present, 1, 0)

            @pl.when(present)
            def _(device=device):
                pl.semaphore_signal(barrier, inc=1, device_id=device, device_id_type=MESH)

        pl.semaphore_wait(barrier, peers)
        for one, sends, _ in direct:
            pl.when(sends)(one.start)

    wide = depth * tile_y
    for layer in range(depth):
        for chunk in range(4):
            source = pl.ds(layer * 512 + chunk * 128, 128)
            lanes = pl.ds(chunk * 128, 128)
            mask = mask_ref[0, :, source].astype(jnp.float32)
            grads = [grad_ref[c, 0, :, source].astype(jnp.float32) for c in range(3)]
            masked = [mask * g for g in grads]
            for q, (c, d) in enumerate(PAIRS):
                rows = pl.ds(q * wide + layer * tile_y, tile_y)
                put_split(masked[c] * grads[d], high_ref, low_ref, rows, lanes)
    table = table_ref[...]
    for q in range(6):
        rows = pl.ds(q * wide, wide)
        total = contract(table, high_ref[rows, :]) + contract(table, low_ref[rows, :])
        value = total[0:32] + total[32:64] + total[64:96]
        out_ref[q, :, pl.ds(step, 1), :] = value[:, None, :]

    @pl.when(step == tile_x - 1)
    def _():
        for k in range(2):
            one, _, receives = direct[k]
            pl.when(receives)(one.wait_recv)
            for other, sends, _ in forwarded[2 * k : 2 * k + 2]:
                pl.when(sends)(other.start)
        for one, _, receives in direct[2:] + forwarded:
            pl.when(receives)(one.wait_recv)
        for one, sends, _ in direct + forwarded:
            pl.when(sends)(one.wait_send)


def load_kernel(
    depth,
    span_y,
    sizes,
    source_ref,
    table_ref,
    *refs,
):
    before_ref, middle_ref, after_ref, beyond_ref, ahead_ref = refs[:5]
    scan_ref, weight_ref, grad_ref, mask_ref, out_ref = refs[5:10]
    wide_ref, near_ref, far_ref, high_ref, low_ref = refs[10:]
    step = pl.program_id(0)
    tile_y = mask_ref.shape[1]
    wide = depth * tile_y

    @pl.when(step == 0)
    def _():
        gx = lax.axis_index("gx")
        gy = lax.axis_index("gy")
        below, over = (gy > 0, gy < sizes[1] - 1)
        begin = 0
        for band, inside in (
            (before_ref, gx > 0),
            (middle_ref, gx >= 0),
            (after_ref, gx < sizes[0] - 1),
        ):

            def convert(i, carry, begin=begin, band=band, inside=inside):
                base = pl.multiple_of((begin + i) * span_y, 8)
                for part, there, offset, count in (
                    (band[i], inside, 0, tile_y),
                    (beyond_ref[begin + i], jnp.logical_and(inside, over), tile_y, 8),
                    (ahead_ref[begin + i], jnp.logical_and(inside, below), tile_y + 8, 8),
                ):
                    value = jnp.where(there, part.astype(jnp.float32), 0.0)
                    wide_ref[pl.ds(base + offset, count), :] = value
                return carry

            lax.fori_loop(0, band.shape[0], convert, 0)
            begin += band.shape[0]

    def fetch(block, carry):
        for inner in range(4):
            y = block * 4 + inner
            for layer in range(depth):
                row = source_ref[(step * tile_y + y) * depth + layer]
                lanes = pl.ds(layer * 512, 512)
                near_ref[pl.ds(y, 1), lanes] = wide_ref[pl.ds(row, 1), lanes]
                far_ref[pl.ds(y, 1), lanes] = wide_ref[pl.ds(row + span_y, 1), lanes]
        return carry

    lax.fori_loop(0, tile_y // 4, fetch, 0)
    for layer in range(depth):
        for chunk in range(4):
            source = pl.ds(layer * 512 + chunk * 128, 128)
            lanes = pl.ds(chunk * 128, 128)
            weight = weight_ref[0, :, source].astype(jnp.float32)
            warped = weight * near_ref[:, source] + (1.0 - weight) * far_ref[:, source]
            image = scan_ref[0, :, source].astype(jnp.float32) - warped
            image = image.astype(jnp.bfloat16).astype(jnp.float32)
            image = image * mask_ref[0, :, source].astype(jnp.float32)
            for c in range(3):
                rows = pl.ds(c * wide + layer * tile_y, tile_y)
                value = image * grad_ref[c, 0, :, source].astype(jnp.float32)
                put_split(value, high_ref, low_ref, rows, lanes)
    table = table_ref[...]
    for c in range(3):
        rows = pl.ds(c * wide, wide)
        total = contract(table, high_ref[rows, :]) + contract(table, low_ref[rows, :])
        value = total[0:8] + total[8:16] + total[16:24]
        out_ref[c, :, pl.ds(step, 1), :] = value[:, None, :]


def solve_kernel(
    sizes,
    tile_y,
    hess_ref,
    load_ref,
    inc_ref,
    res_ref,
    field_ref,
    image_ref,
    out_x,
    out_y,
    out_c,
    in_x,
    in_y,
    in_c,
    own_x,
    got_x,
    own_y,
    got_y,
    send_sems,
    recv_sems,
    send_x,
    recv_x,
    send_y,
    recv_y,
):
    n_gx, n_gy = sizes
    tile_x, width = (hess_ref.shape[2], hess_ref.shape[3])
    gx = lax.axis_index("gx")
    gy = lax.axis_index("gy")
    in_x[...] = jnp.zeros_like(in_x)
    in_y[...] = jnp.zeros_like(in_y)
    in_c[...] = jnp.zeros_like(in_c)

    barrier = pltpu.get_barrier_semaphore()
    for k in range(1, n_gx):
        pl.semaphore_signal(barrier, inc=1, device_id=((gx + k) % n_gx, gy), device_id_type=MESH)
    for k in range(1, n_gy):
        pl.semaphore_signal(barrier, inc=1, device_id=(gx, (gy + k) % n_gy), device_id_type=MESH)
    low = jnp.logical_and(gx > 0, gy > 0)
    high = jnp.logical_and(gx < n_gx - 1, gy < n_gy - 1)

    @pl.when(low)
    def _():
        pl.semaphore_signal(barrier, inc=1, device_id=(gx - 1, gy - 1), device_id_type=MESH)

    @pl.when(high)
    def _():
        pl.semaphore_signal(barrier, inc=1, device_id=(gx + 1, gy + 1), device_id_type=MESH)

    corners = jnp.where(low, 1, 0) + jnp.where(high, 1, 0)
    pl.semaphore_wait(barrier, n_gx - 1 + n_gy - 1 + corners)

    lane = lax.broadcasted_iota(jnp.int32, (1, tile_x, width), 2)
    row = lax.broadcasted_iota(jnp.int32, (1, tile_x, width), 1)
    in_tile = lane % tile_y
    first_y = in_tile == 0
    last_y = in_tile == tile_y - 1
    first_x = row == 0
    last_x = row == tile_x - 1
    topmost = lane >= width - tile_y
    above = lane >= tile_y

    def copies(phase, dx, dy):
        def make(k, src, dst, target):
            return pltpu.make_async_remote_copy(
                src_ref=src.at[phase],
                dst_ref=dst.at[phase],
                send_sem=send_sems.at[phase, k],
                recv_sem=recv_sems.at[phase, k],
                device_id=target,
                device_id_type=MESH,
            )

        up = dx > 0
        send_gx, recv_gx = (gx < n_gx - 1, gx > 0) if up else (gx > 0, gx < n_gx - 1)
        send_gy, recv_gy = (gy < n_gy - 1, gy > 0) if up else (gy > 0, gy < n_gy - 1)
        return [
            (make(0, out_x, in_x, (gx + dx, gy)), send_gx, recv_gx),
            (make(1, out_y, in_y, (gx, gy + dy)), send_gy, recv_gy),
            (
                make(2, out_c, in_c, (gx + dx, gy + dy)),
                jnp.logical_and(send_gx, send_gy),
                jnp.logical_and(recv_gx, recv_gy),
            ),
        ]

    def start(phase, step):
        for copy, sends, _ in copies(phase, step, step):
            pl.when(sends)(copy.start)

    def arrive(phase, step):
        for copy, _, receives in copies(phase, step, step):
            pl.when(receives)(copy.wait_recv)

    def finish(phase, step):
        for copy, sends, _ in copies(phase, step, step):
            pl.when(sends)(copy.wait_send)

    def roll(value, shift, axis):
        return pltpu.roll(value, shift % value.shape[axis], axis)

    def shift_x(value):
        return jnp.where(first_x, 0.0, roll(value, 1, 1))

    def collect(phase, meanwhile):
        folded = {}
        for i in range(2):
            for j in range(2):
                under = image_ref[pl.ds((4 * i + 2 * j) * 3, 3)]
                over = image_ref[pl.ds((4 * i + 2 * j + 1) * 3, 3)]
                main = under + jnp.where(above, roll(over, tile_y, 2), 0.0)
                top = jnp.where(topmost, over, 0.0)
                folded[i, j] = jnp.concatenate([main, top], axis=0)
        kept, passed = ([], [])
        for i in range(2):
            kept.append(folded[i, 0] + jnp.where(first_y, 0.0, roll(folded[i, 1], 1, 2)))
            passed.append(jnp.where(first_y, roll(folded[i, 1], 1 - tile_y, 2), 0.0))
        out_x[phase] = kept[1][:, tile_x - 8 :, :]
        out_y[phase] = passed[0] + shift_x(passed[1])
        out_c[phase] = passed[1][:, tile_x - 8 :, :]
        start(phase, 1)
        total = kept[0] + shift_x(kept[1])
        meanwhile()
        arrive(phase, 1)
        edge = in_x[phase][:, 7:8, :] + in_c[phase][:, 7:8, :]
        return total + in_y[phase] + jnp.where(first_x, edge, 0.0)

    def spread(phase, field, meanwhile):
        turned = roll(field, tile_y - 1, 2)
        out_x[phase] = field[:, 0:8, :]
        out_y[phase] = turned
        out_c[phase] = turned[:, 0:8, :]
        start(phase, -1)
        meanwhile()
        next_x = roll(field, -1, 1)
        next_y = roll(field, -1, 2)

        def place(i, j, value):
            main, top = (value[0:3], value[3:6])
            field_ref[pl.ds((4 * i + 2 * j) * 3, 3)] = main
            field_ref[pl.ds((4 * i + 2 * j + 1) * 3, 3)] = jnp.where(
                topmost, top, roll(main, -tile_y, 2)
            )

        place(0, 0, field)
        arrive(phase, -1)
        side = in_x[phase]
        next_x = jnp.where(last_x, side[:, 0:1, :], next_x)
        next_y = jnp.where(last_y, in_y[phase], next_y)
        corner = jnp.where(last_y[:, 0:8], in_c[phase], roll(side, -1, 2))
        both = jnp.where(last_x, corner[:, 0:1, :], roll(next_y, -1, 1))
        place(1, 0, next_x)
        place(0, 1, next_y)
        place(1, 1, both)

    def apply():
        for n, (i, j, l) in enumerate(NODES):
            for c in range(3):
                total = None
                for m, (p, q, r) in enumerate(NODES):
                    kind = (i + p) * 9 + (j + q) * 3 + l + r
                    for d in range(3):
                        term = hess_ref[PAIR_OF[c, d], kind] * field_ref[3 * m + d]
                        total = term if total is None else total + term
                image_ref[3 * n + c] = total

    def exchange(own, got, sends, receives, slot, index, count, target):
        return [
            pltpu.make_async_remote_copy(
                src_ref=own.at[slot],
                dst_ref=got.at[slot, k - 1],
                send_sem=sends.at[slot, k - 1],
                recv_sem=receives.at[slot, k - 1],
                device_id=target((index + k) % count),
                device_id_type=MESH,
            )
            for k in range(1, count)
        ]

    def along_x(slot):
        return exchange(own_x, got_x, send_x, recv_x, slot, gx, n_gx, lambda t: (t, gy))

    def along_y(slot):
        return exchange(own_y, got_y, send_y, recv_y, slot, gy, n_gy, lambda t: (gx, t))

    def total_of(copies, own, got, slot, index, count):
        for copy in copies:
            copy.wait_recv()
        others = [got[slot, k - 1] for k in range(1, count)]
        return in_order(index, count, own[slot], others)

    def in_order(index, count, mine, others):
        total = jnp.zeros_like(mine)
        for source in range(count):
            value = jnp.where(index == source, mine, 0.0)
            for k in range(1, count):
                value = jnp.where((index - k + count) % count == source, others[k - 1], value)
            total = total + value
        return total

    def open_products(slot, vector, image):
        one = jnp.sum(jnp.sum(vector * vector, axis=0), axis=0, keepdims=True)
        two = jnp.sum(jnp.sum(vector * image, axis=0), axis=0, keepdims=True)
        line = lax.broadcasted_iota(jnp.int32, (8, width), 0)
        own_x[slot] = jnp.where(line == 0, one, jnp.where(line == 1, two, 0.0))
        for copy in along_x(slot):
            copy.start()

    def pass_products(slot):
        own_y[slot] = total_of(along_x(slot), own_x, got_x, slot, gx, n_gx)
        for copy in along_y(slot):
            copy.start()

    def close_products(slot):
        total = total_of(along_y(slot), own_y, got_y, slot, gy, n_gy)
        return (
            jnp.sum(total[0:1], axis=1, keepdims=True)[None],
            jnp.sum(total[1:2], axis=1, keepdims=True)[None],
        )

    def nothing():
        return None

    def operate(phase, field, during_spread=nothing, during_collect=nothing):
        spread(phase, field, during_spread)
        apply()
        return collect(phase + 1, during_collect) + tikhonov * field

    for c in range(3):
        for n in range(8):
            image_ref[3 * n + c] = load_ref[c, n]
    rhs = collect(0, nothing)
    increment = jnp.zeros_like(rhs)
    residual = rhs
    image = operate(1, residual)
    for sweep in range(ITERS):
        if sweep + 1 < ITERS:
            second = operate(
                2 * sweep + 3,
                image,
                lambda: open_products(sweep, residual, image),
                lambda: pass_products(sweep),
            )
        else:
            open_products(sweep, residual, image)
            pass_products(sweep)
        norm_next, product = close_products(sweep)
        if sweep == 0:
            step_size = norm_next / product
            direction, along = (residual, image)
        else:
            factor = norm_next / norm_now
            step_size = norm_next / (product - factor * norm_next / step_size)
            direction = residual + factor * direction
            along = image + factor * along
        norm_now = norm_next
        increment = increment + step_size * direction
        residual = residual - step_size * along
        if sweep + 1 < ITERS:
            deep = second if sweep == 0 else second + factor * deep
            image = image - step_size * deep
    inc_ref[...] = increment
    res_ref[...] = residual
    finish(0, 1)
    for sweep in range(ITERS):
        finish(2 * sweep + 1, -1)
        finish(2 * sweep + 2, 1)
        for copy in along_x(sweep) + along_y(sweep):
            copy.wait_send()


def per_device(
    reference_scan, ref_gradient, deformed_scan, interp_weights, sample_mask, block_list, offsets
):
    tile_x, tile_y, column = reference_scan.shape
    depth = column // 512
    width = depth * tile_y
    square_table, shape_table = tables()

    n_gx, n_gy = (lax.axis_size("gx"), lax.axis_size("gy"))
    span_x, span_y = (tile_x + 2 * BOUND + 1, tile_y + 16)
    pos_x = jnp.arange(tile_x)[:, None, None]
    pos_y = jnp.arange(tile_y)[None, :, None]
    source = (pos_x + offsets[0] + BOUND) * span_y + (pos_y + offsets[1] + span_y) % span_y

    voxels = pl.BlockSpec((1, tile_y, column), lambda x: (x, 0, 0))
    gradients = pl.BlockSpec((3, 1, tile_y, column), lambda x: (0, x, 0, 0))
    vmem = pl.BlockSpec(memory_space=pltpu.VMEM)
    size = tile_x * tile_y * column
    anywhere = pl.BlockSpec(memory_space=pl.ANY)
    hessian, before, after, beyond, ahead = pl.pallas_call(
        functools.partial(hessian_kernel, depth, (n_gx, n_gy)),
        grid=(tile_x,),
        out_shape=[jax.ShapeDtypeStruct((6, 32, tile_x, width), jnp.float32)]
        + [
            jax.ShapeDtypeStruct(extent + (column,), jnp.bfloat16)
            for extent in (
                (BOUND, tile_y),
                (BOUND + 1, tile_y),
                (tile_x + 2 * BOUND + 1, 8),
                (tile_x + 2 * BOUND + 1, 8),
            )
        ],
        in_specs=[pl.BlockSpec((96, 512), lambda x: (0, 0)), gradients, voxels, anywhere],
        out_specs=[pl.BlockSpec((6, 32, tile_x, width), lambda x: (0, 0, 0, 0))] + [anywhere] * 4,
        scratch_shapes=[pltpu.VMEM((6 * width, 512), jnp.bfloat16)] * 2
        + [pltpu.SemaphoreType.DMA((8,))] * 2,
        compiler_params=pltpu.CompilerParams(collective_id=1, has_side_effects=True),
        cost_estimate=pl.CostEstimate(
            flops=size * 6 * 2 * 256, bytes_accessed=size * 10, transcendentals=0
        ),
        name="hessian",
    )(square_table, ref_gradient, sample_mask, deformed_scan)
    pieces = [before, deformed_scan, after, beyond, ahead]
    load = pl.pallas_call(
        functools.partial(load_kernel, depth, span_y, (n_gx, n_gy)),
        grid=(tile_x,),
        out_shape=jax.ShapeDtypeStruct((3, 8, tile_x, width), jnp.float32),
        in_specs=[
            pl.BlockSpec(memory_space=pltpu.SMEM),
            pl.BlockSpec((32, 512), lambda x: (0, 0)),
        ]
        + [pl.BlockSpec(piece.shape, lambda x: (0, 0, 0)) for piece in pieces]
        + [
            voxels,
            voxels,
            gradients,
            voxels,
        ],
        out_specs=pl.BlockSpec((3, 8, tile_x, width), lambda x: (0, 0, 0, 0)),
        scratch_shapes=[
            pltpu.VMEM((span_x * span_y, column), jnp.float32),
            pltpu.VMEM((tile_y, column), jnp.float32),
            pltpu.VMEM((tile_y, column), jnp.float32),
            pltpu.VMEM((3 * width, 512), jnp.bfloat16),
            pltpu.VMEM((3 * width, 512), jnp.bfloat16),
        ],
        name="load",
    )(
        source.reshape(-1),
        shape_table,
        *pieces,
        reference_scan,
        interp_weights,
        ref_gradient,
        sample_mask,
    )
    n_gx, n_gy = (lax.axis_size("gx"), lax.axis_size("gy"))
    phases = 2 * ITERS + 1
    part = jax.ShapeDtypeStruct((6, tile_x, width), jnp.float32)
    dma = pltpu.SemaphoreType.DMA
    increment, residual = pl.pallas_call(
        functools.partial(solve_kernel, (n_gx, n_gy), tile_y),
        out_shape=(part, part),
        in_specs=[vmem, vmem],
        out_specs=(vmem, vmem),
        scratch_shapes=[
            pltpu.VMEM((24, tile_x, width), jnp.float32),
            pltpu.VMEM((24, tile_x, width), jnp.float32),
        ]
        + [
            pltpu.VMEM((phases, 6, rows, width), jnp.float32)
            for rows in (8, tile_x, 8, 8, tile_x, 8)
        ]
        + [
            pltpu.VMEM((ITERS, 8, width), jnp.float32),
            pltpu.VMEM((ITERS, n_gx - 1, 8, width), jnp.float32),
            pltpu.VMEM((ITERS, 8, width), jnp.float32),
            pltpu.VMEM((ITERS, n_gy - 1, 8, width), jnp.float32),
            dma((phases, 3)),
            dma((phases, 3)),
            dma((ITERS, n_gx - 1)),
            dma((ITERS, n_gx - 1)),
            dma((ITERS, n_gy - 1)),
            dma((ITERS, n_gy - 1)),
        ],
        compiler_params=pltpu.CompilerParams(collective_id=0, has_side_effects=True),
        name="solve",
    )(hessian, load)

    def nodal(value):
        main = jnp.transpose(value[:3].reshape(3, tile_x, depth, tile_y), (0, 1, 3, 2))
        return jnp.concatenate([main, value[3:, :, width - tile_y :, None]], axis=3)

    return (nodal(increment), nodal(residual))


def solution(mesh):
    return jax.shard_map(
        per_device,
        mesh=mesh,
        in_specs=(
            P("gx", "gy", None),
            P(None, "gx", "gy", None),
            P("gx", "gy", None),
            P("gx", "gy", None),
            P("gx", "gy", None),
            P("gx", "gy"),
            P(None, "gx", "gy", None),
        ),
        out_specs=(P(None, "gx", "gy", None), P(None, "gx", "gy", None)),
        check_vma=False,
    )
```

profile of v0, /device:TPU:0, one launch (start us, length us, event | category | flops | bytes accessed | tf_op | source)
XLA Modules:
  0.0 111.8 jit_solution(16705848866661203029)
XLA Ops:
  0.6 0.1 pad.12.clone
  1.3 0.7 maximum_maximum_fusion.table_ref
  2.0 0.1 stack.4
  2.1 0.6 pad_maximum_fusion.2.table_ref
  2.8 0.8 fusion.73
  3.6 0.2 copy.13
  3.8 0.2 squeeze.7
  3.9 0.2 copy.12
  4.1 0.2 squeeze.6
  4.3 0.2 add.1419
  4.5 0.2 add.1414
  4.6 0.6 fusion.2.source_ref
  5.3 31.5 %hessian.1 = (f32[6,32,16,128]{3,2,1,0:T(8,128)}, bf16[4,32,2048]{2,1,0:T(8,128)(2,1)}, bf16[5,32,2048]{2,1,0:T(8,128)(2,1)}, bf16[25,8,2048]{2,1,0:T(8,128)(2,1)}, bf16[25,8,2048]{2,1,0:T(8,128)(2,1)}) custom-call(bf16[96,512]{1,0:T(8,128)(2,1)} %pad_maximum_fusion.2.table_ref, bf16[3,16,32,2048]{3,2,1,0:T(8,128)(2,1)} %refs_7_.1, s32[16,32,2048]{2,1,0:T(8,128)} %refs_8_.1, ...), custom_call_target="tpu_custom_call" | custom-call | flops 3221225472 | bytes 10485760 | tf_op jit(solution)/shard_map/hessian/pallas_call | solution.py:557
  36.8 24.4 %load.1.load_ref = f32[3,8,16,128]{3,2,1,0:T(8,128)} custom-call(s32[2048]{0:T(1024)} %fusion.2.source_ref, bf16[32,512]{1,0:T(8,128)(2,1)} %maximum_maximum_fusion.table_ref, bf16[4,32,2048]{2,1,0:T(8,128)(2,1)} %get-tuple-element.10.refs_0_, bf16[16,32,2048]{2,1,0:T(8,128)(2,1)} %refs_1_.1, bf16[5,32,2048]{2,1,0:T(8,128)(2,1)} %get-tuple-element.11.refs_2_, ...), custom_call_target="tpu_custom_call" | custom-call | tf_op jit(solution)/shard_map/load/pallas_call | solution.py:581
  61.2 45.9 %solve.1 = (f32[6,16,128]{2,1,0:T(8,128)}, f32[6,16,128]{2,1,0:T(8,128)}) custom-call(f32[6,32,16,128]{3,2,1,0:T(8,128)} %get-tuple-element.9.hess_ref, f32[3,8,16,128]{3,2,1,0:T(8,128)} %load.1.load_ref), custom_call_target="tpu_custom_call" | custom-call | tf_op jit(solution)/shard_map/solve/pallas_call | solution.py:618
  107.1 0.8 slice_bitcast_fusion.1
  107.9 0.7 slice.20
  108.7 0.8 slice_bitcast_fusion
  109.5 0.7 slice.22
  110.2 0.1 reshape.363
  110.3 0.7 pad_maximum_fusion.1
  111.0 0.1 reshape.362
  111.1 0.7 pad_maximum_fusion
  (27 shorter events, 0.5 us)
where the time goes:
time: 113 us; the launch traced here: 112 us
  Pallas kernels  102 us (90%)
  local copies, waits for them, and re-layouts  5.42 us (5%)
  other arithmetic  3.71 us (3%)
    pallas_call x1, Pallas kernels, per_device(): pl.pallas_call(functools.partial(solve_kernel, (n_gx, n_gy), tile_y), out...  45.9 us
    pallas_call x1, Pallas kernels, per_device(): pl.pallas_call(functools.partial(hessian_kernel, depth, (n_gx, n_gy)), gr...  31.5 us
    pallas_call x1, Pallas kernels, per_device(): pl.pallas_call(functools.partial(load_kernel, depth, span_y, (n_gx, n_gy)...  24.4 us

commit v1 on v0

v1 whole, which is shorter than its diff:
```python
import functools

import jax
import jax.numpy as jnp
import ml_dtypes
import numpy as np
from jax import lax
from jax.experimental import pallas as pl
from jax.experimental.pallas import tpu as pltpu
from jax.sharding import PartitionSpec as P

BOUND = 4
ITERS = 3
PHASES = ITERS + 1
EDGE = 8

tikhonov = 8.0
UNIT = 64.0

NODES = [(n >> 2 & 1, n >> 1 & 1, n & 1) for n in range(8)]
PAIRS = [(c, d) for c in range(3) for d in range(c, 3)]
PAIR_OF = {(c, d): PAIRS.index((min(c, d), max(c, d))) for c in range(3) for d in range(3)}
MESH = pl.DeviceIdType.MESH


def split(table, count):
    parts = []
    for _ in range(count):
        part = table.astype(ml_dtypes.bfloat16)
        parts.append(part)
        table = table - part.astype(np.float32)
    return parts


def tables():
    voxel = np.arange(512)
    coords = [
        ((voxel // 64).astype(np.float32) + np.float32(0.5)) / np.float32(8.0),
        ((voxel // 8 % 8).astype(np.float32) + np.float32(0.5)) / np.float32(8.0),
        ((voxel % 8).astype(np.float32) + np.float32(0.5)) / np.float32(8.0),
    ]
    linear = [[np.float32(1.0) - t, t] for t in coords]
    quad = [[s[0] * s[0], s[0] * s[1], s[1] * s[1]] for s in linear]
    shapes = np.stack([linear[0][i] * linear[1][j] * linear[2][l] for i, j, l in NODES])
    squares = np.stack(
        [quad[0][a] * quad[1][b] * quad[2][c] for a in range(3) for b in range(3) for c in range(3)]
    )
    squares = np.pad(squares, ((0, 5), (0, 0))) / np.float32(UNIT)
    square_table = np.concatenate(split(squares.astype(np.float32), 2), axis=0)
    shape_table = np.concatenate(split(shapes.astype(np.float32), 2), axis=0)
    return (square_table, shape_table)


def contract(table, part):
    return lax.dot_general(
        table, part, (((1,), (1,)), ((), ())), preferred_element_type=jnp.float32
    )


def row_of(step, tile_x):
    turn = jnp.maximum(step - tile_x, 0)
    return jnp.where(turn < tile_x - BOUND, turn + BOUND, tile_x - 1 - turn)


def step_kernel(
    sizes,
    tile_x,
    tile_y,
    depth,
    source_ref,
    square_ref,
    shape_ref,
    grad_ref,
    mask_ref,
    own_ref,
    image_ref,
    weight_ref,
    scan_ref,
    inc_ref,
    res_ref,
    before_ref,
    after_ref,
    beyond_ref,
    ahead_ref,
    wide_ref,
    masked_ref,
    part_ref,
    fetched_ref,
    high_ref,
    low_ref,
    hess_ref,
    load_ref,
    field_ref,
    value_ref,
    out_e,
    out_w,
    out_n,
    out_s,
    in_w,
    in_e,
    in_s,
    in_n,
    in_sw,
    in_ne,
    in_nw,
    in_se,
    own_x,
    got_x,
    own_y,
    got_y,
    halo_send,
    halo_recv,
    send_sems,
    recv_sems,
    send_x,
    recv_x,
    send_y,
    recv_y,
):
    step = pl.program_id(0)
    n_gx, n_gy = sizes
    gx = lax.axis_index("gx")
    gy = lax.axis_index("gy")
    not_first_x, not_last_x = (gx > 0, gx < n_gx - 1)
    not_first_y, not_last_y = (gy > 0, gy < n_gy - 1)
    both = jnp.logical_and
    wide = depth * tile_y
    span_x = tile_x + 2 * BOUND + 1
    stride_y = depth * span_x * 4

    def remote(source, target, sends, receives, device):
        return pltpu.make_async_remote_copy(
            src_ref=source,
            dst_ref=target,
            send_sem=sends,
            recv_sem=receives,
            device_id=device,
            device_id_type=MESH,
        )

    def halo(k, source, target, device):
        return remote(source, target, halo_send.at[k], halo_recv.at[k], device)

    every = slice(None)
    low_y, high_y = (pl.ds(0, EDGE), pl.ds(tile_y - EDGE, EDGE))
    near_y, far_y = ((gx, gy - 1), (gx, gy + 1))
    middle = pl.ds(BOUND, tile_x)

    def y_copies():
        return [
            (halo(0, scan_ref.at[every, low_y], beyond_ref.at[middle], near_y), not_first_y, not_last_y),
            (halo(1, scan_ref.at[every, high_y], ahead_ref.at[middle], far_y), not_last_y, not_first_y),
        ]

    def after_copy(k):
        return (halo(2 + k, scan_ref.at[k], after_ref.at[k], (gx - 1, gy)), not_first_x, not_last_x)

    def before_copy(k):
        source = scan_ref.at[tile_x - BOUND + k]
        return (
            halo(3 + BOUND + k, source, before_ref.at[k], (gx + 1, gy)),
            not_last_x,
            not_first_x,
        )

    def corner_copies(first, band, k, row, present):
        return [
            (
                halo(first, band.at[k, low_y], beyond_ref.at[row], near_y),
                both(present, not_first_y),
                both(present, not_last_y),
            ),
            (
                halo(first + 1, band.at[k, high_y], ahead_ref.at[row], far_y),
                both(present, not_last_y),
                both(present, not_first_y),
            ),
        ]

    def after_corners(k):
        first = 3 + 2 * BOUND + 2 * k
        return corner_copies(first, after_ref, k, BOUND + tile_x + k, not_last_x)

    def before_corners(k):
        first = 5 + 4 * BOUND + 2 * k
        return corner_copies(first, before_ref, k, k, not_first_x)

    def begin(copies):
        for one, sends, _ in copies:
            pl.when(sends)(one.start)

    def arrive(copies):
        for one, _, receives in copies:
            pl.when(receives)(one.wait_recv)

    def sent(copies):
        for one, sends, _ in copies:
            pl.when(sends)(one.wait_send)

    def put_wide(value, at_x, at_y):
        count = value.shape[0]
        for layer in range(depth):
            for chunk in range(4):
                lanes = slice(layer * 512 + chunk * 128, layer * 512 + chunk * 128 + 128)
                start = at_y * stride_y + (layer * span_x + at_x) * 4 + chunk
                wide_ref[pl.ds(start, count, stride=stride_y), :] = value[:, lanes]

    def put_sides(row, inside):
        value = beyond_ref[row].astype(jnp.float32)[0:BOUND]
        put_wide(jnp.where(both(inside, not_last_y), value, 0.0), row, BOUND + tile_y)
        value = ahead_ref[row].astype(jnp.float32)[EDGE - BOUND :]
        put_wide(jnp.where(both(inside, not_first_y), value, 0.0), row, 0)

    def put_band(band, k, row, inside):
        for first in range(0, tile_y, 16):
            value = band[k, pl.ds(first, 16), :].astype(jnp.float32)
            put_wide(jnp.where(inside, value, 0.0), row, BOUND + first)
        put_sides(row, inside)

    @pl.when(step == 0)
    def _():
        for buffer in (in_w, in_e, in_s, in_n, in_sw, in_ne, in_nw, in_se):
            buffer[...] = jnp.zeros_like(buffer)
        for buffer in (out_e, out_w, out_n, out_s):
            buffer[...] = jnp.zeros_like(buffer)
        barrier = pltpu.get_barrier_semaphore()
        for k in range(1, n_gx):
            pl.semaphore_signal(
                barrier, inc=1, device_id=((gx + k) % n_gx, gy), device_id_type=MESH
            )
        for k in range(1, n_gy):
            pl.semaphore_signal(
                barrier, inc=1, device_id=(gx, (gy + k) % n_gy), device_id_type=MESH
            )
        corners = 0
        for dx, there_x in ((-1, not_first_x), (1, not_last_x)):
            for dy, there_y in ((-1, not_first_y), (1, not_last_y)):
                present = both(there_x, there_y)
                corners = corners + jnp.where(present, 1, 0)

                @pl.when(present)
                def _(dx=dx, dy=dy):
                    pl.semaphore_signal(
                        barrier, inc=1, device_id=(gx + dx, gy + dy), device_id_type=MESH
                    )

        pl.semaphore_wait(barrier, n_gx - 1 + n_gy - 1 + corners)
        begin(y_copies())
        begin([after_copy(k) for k in range(BOUND + 1)])
        begin([before_copy(BOUND - 1 - k) for k in range(BOUND)])

    @pl.when(step < tile_x)
    def _():
        for first in range(0, tile_y, 16):
            value = own_ref[0, pl.ds(first, 16), :].astype(jnp.float32)
            put_wide(value, BOUND + step, BOUND + first)
        for layer in range(depth):
            lanes = pl.ds(layer * 512, 512)
            mask = mask_ref[0, :, lanes].astype(jnp.float32).astype(jnp.bfloat16)
            grads = [grad_ref[c, 0, :, lanes] for c in range(3)]
            masked = [mask * g for g in grads]
            for c in range(3):
                masked_ref[step, c, :, lanes] = masked[c]
            for q, (c, d) in enumerate(PAIRS):
                part_ref[pl.ds(q * wide + layer * tile_y, tile_y), :] = masked[c] * grads[d]
        table = square_ref[...]
        for q in range(6):
            total = contract(table, part_ref[pl.ds(q * wide, wide), :])
            value = total[0:32] + total[32:64]
            for first in range(0, 32, 8):
                rows = pl.ds((q * 32 + first) * tile_x + step, 8, stride=tile_x)
                hess_ref[rows, :] = value[first : first + 8]

    turn = step - tile_x

    @pl.when(turn == 0)
    def _():
        arrive(y_copies())

        def convert(i, carry):
            put_sides(BOUND + i, gx >= 0)
            return carry

        lax.fori_loop(0, tile_x, convert, 0)

    head = tile_x - 2 * BOUND - 1
    turned = tile_x - BOUND

    @pl.when(both(turn >= head - 2, turn < turned - 2))
    def _():
        k = turn - (head - 2)
        arrive([after_copy(k)])
        begin(after_corners(k))

    @pl.when(both(turn >= turned - 2, turn < tile_x - 2))
    def _():
        k = tile_x - 3 - turn
        arrive([before_copy(k)])
        begin(before_corners(k))

    @pl.when(both(turn >= head, turn < turned))
    def _():
        k = turn - head
        arrive(after_corners(k))
        put_band(after_ref, k, BOUND + tile_x + k, not_last_x)

    @pl.when(turn >= turned)
    def _():
        k = tile_x - 1 - turn
        arrive(before_corners(k))
        put_band(before_ref, k, k, not_first_x)

    @pl.when(turn >= 0)
    def _():
        x = row_of(step, tile_x)

        def fetch(block, carry):
            for inner in range(4):
                y = block * 4 + inner
                for layer in range(depth):
                    row = source_ref[(x * tile_y + y) * depth + layer]
                    rows = pl.ds(pl.multiple_of((y * depth + layer) * 8, 8), 8)
                    fetched_ref[rows, :] = wide_ref[pl.ds(row, 8), :]
            return carry

        lax.fori_loop(0, tile_y // 4, fetch, 0)
        for layer in range(depth):
            for chunk in range(4):
                lanes = pl.ds(layer * 512 + chunk * 128, 128)
                part = pl.ds(chunk * 128, 128)
                near = fetched_ref[pl.ds(layer * 8 + chunk, tile_y, stride=8 * depth), :]
                far = fetched_ref[pl.ds(layer * 8 + 4 + chunk, tile_y, stride=8 * depth), :]
                weight = weight_ref[0, :, lanes].astype(jnp.float32)
                warped = weight * near + (1.0 - weight) * far
                image = image_ref[0, :, lanes].astype(jnp.float32) - warped
                image = image.astype(jnp.bfloat16).astype(jnp.float32)
                for c in range(3):
                    rows = pl.ds(c * wide + layer * tile_y, tile_y)
                    value = image * masked_ref[x, c, :, lanes].astype(jnp.float32)
                    high = value.astype(jnp.bfloat16)
                    high_ref[rows, part] = high
                    low_ref[rows, part] = (value - high.astype(jnp.float32)).astype(jnp.bfloat16)
        table = shape_ref[...]
        for c in range(3):
            rows = pl.ds(c * wide, wide)
            total = contract(table, high_ref[rows, :]) + contract(table, low_ref[rows, :])
            load_ref[pl.ds(c * 8 * tile_x + x, 8, stride=tile_x), :] = total[0:8] + total[8:16]

    @pl.when(step == 2 * tile_x - 1)
    def _():
        width = wide
        lane = lax.broadcasted_iota(jnp.int32, (tile_x, width), 1)
        row = lax.broadcasted_iota(jnp.int32, (tile_x, width), 0)
        in_tile = lane % tile_y
        first_y = in_tile == 0
        last_y = in_tile == tile_y - 1
        first_x = row == 0
        last_x = row == tile_x - 1
        topmost = lane >= width - tile_y
        above = lane >= tile_y
        first_8, last_8 = (first_y[0:8], last_y[0:8])
        turn_y = tile_y - 1
        body, tail = (pl.ds(0, tile_x), pl.ds(tile_x, 8))
        upper, lower = (pl.ds(0, 8), pl.ds(8, 8))

        def roll(value, shift, axis):
            return pltpu.roll(value, shift % value.shape[axis], axis)

        def shift_x(value):
            return jnp.where(first_x, 0.0, roll(value, 1, 0))

        def copies(phase):
            table = [
                (out_e, None, in_w, 1, 0),
                (out_n, None, in_s, 0, 1),
                (out_e, lower, in_sw, 1, 1),
                (out_w, None, in_e, -1, 0),
                (out_s, None, in_n, 0, -1),
                (out_w, upper, in_ne, -1, -1),
                (out_e, upper, in_nw, 1, -1),
                (out_w, lower, in_se, -1, 1),
            ]
            if phase == PHASES - 1:
                table = table[:3]
            found = []
            for k, (src, rows, dst, dx, dy) in enumerate(table):
                send_ok, recv_ok = (gx >= 0, gx >= 0)
                if dx:
                    send_ok = not_last_x if dx > 0 else not_first_x
                    recv_ok = not_first_x if dx > 0 else not_last_x
                if dy:
                    send_ok = both(send_ok, not_last_y if dy > 0 else not_first_y)
                    recv_ok = both(recv_ok, not_first_y if dy > 0 else not_last_y)
                source = src.at[phase] if rows is None else src.at[phase, rows]
                one = remote(
                    source,
                    dst.at[phase],
                    send_sems.at[phase, k],
                    recv_sems.at[phase, k],
                    (gx + dx, gy + dy),
                )
                found.append((one, send_ok, recv_ok))
            return found

        def assemble(phase, partial, meanwhile):
            folded = {}
            for i in range(2):
                for j in range(2):
                    found = []
                    for c in range(3):
                        under = partial((4 * i + 2 * j) * 3 + c)
                        over = partial((4 * i + 2 * j + 1) * 3 + c)
                        found.append(under + jnp.where(above, roll(over, tile_y, 1), 0.0))
                        folded[i, j, 3 + c] = jnp.where(topmost, over, 0.0)
                    for c in range(3):
                        folded[i, j, c] = found[c]
            total, right = ([], [])
            north = jnp.zeros((tile_x, width), jnp.float32)
            south = jnp.zeros((tile_x, width), jnp.float32)
            for a in range(6):
                kept = [
                    folded[i, 0, a] + jnp.where(first_y, 0.0, roll(folded[i, 1, a], 1, 1))
                    for i in range(2)
                ]
                mine = kept[0] + shift_x(kept[1])
                side = folded[0, 1, a] + shift_x(folded[1, 1, a])
                edge_x = kept[1][tile_x - 1 :]
                edge_c = folded[1, 1, a][tile_x - 1 :]
                out_e[phase, a : a + 1, :] = edge_x
                out_e[phase, 8 + a : 9 + a, :] = edge_c
                out_w[phase, a : a + 1, :] = mine[0:1]
                out_w[phase, 8 + a : 9 + a, :] = side[0:1]
                out_n[phase, tile_x + a : tile_x + a + 1, :] = edge_c
                out_s[phase, tile_x + a : tile_x + a + 1, :] = edge_x
                north = jnp.where(in_tile == a, roll(side, a + 1, 1), north)
                south = jnp.where(in_tile == a, roll(mine, a, 1), south)
                total.append(mine)
                right.append(side)
            out_n[phase, body, :] = north
            out_s[phase, body, :] = south
            begin(copies(phase))
            meanwhile()
            arrive(copies(phase))
            line = in_w[phase, upper, :] + jnp.where(
                first_8, roll(in_sw[phase], -turn_y, 1), 0.0
            )
            from_s = in_s[phase, body, :]
            whole = [
                total[a]
                + jnp.where(first_x, line[a : a + 1], 0.0)
                + jnp.where(first_y, roll(from_s, -(tile_y + a), 1), 0.0)
                for a in range(6)
            ]
            if phase == PHASES - 1:
                return whole
            side_x = in_s[phase, tail, :] + in_se[phase]
            side_x = jnp.where(first_8, roll(side_x, -turn_y, 1), 0.0)
            side_x = jnp.where(not_last_x, out_e[phase, upper, :] + in_e[phase, upper, :] + side_x, 0.0)
            line = in_w[phase, lower, :] + roll(in_nw[phase], turn_y, 1)
            corner = in_n[phase, tail, :] + in_ne[phase]
            corner = out_e[phase, lower, :] + in_e[phase, lower, :] + roll(corner, turn_y, 1)
            corner = jnp.where(both(not_last_x, not_last_y), corner, 0.0)
            corner = jnp.where(last_8, corner, roll(side_x, -1, 1))
            from_n = in_n[phase, body, :]
            for a in range(6):
                side = right[a] + jnp.where(first_x, line[a : a + 1], 0.0)
                side = side + roll(from_n, turn_y - a, 1)
                side = jnp.where(not_last_y, side, 0.0)
                next_x = jnp.where(last_x, side_x[a : a + 1], roll(whole[a], -1, 0))
                next_y = jnp.where(last_y, side, roll(whole[a], -1, 1))
                next_c = jnp.where(last_x, corner[a : a + 1], roll(next_y, -1, 0))
                for k, value in enumerate((whole[a], next_y, next_x, next_c)):
                    if a < 3:
                        field_ref[6 * k + a] = value
                        field_ref[6 * k + 3 + a] = roll(value, -tile_y, 1)
                    else:
                        above_it = field_ref[6 * k + a]
                        field_ref[6 * k + a] = jnp.where(topmost, value, above_it)
            return whole

        def apply():
            for half in range(0, tile_x, 8):
                rows = pl.ds(half, 8)
                fields = [field_ref[k, rows, :] for k in range(24)]
                for n, (i, j, l) in enumerate(NODES):
                    for c in range(3):
                        total = None
                        for m, (p, q, r) in enumerate(NODES):
                            kind = (i + p) * 9 + (j + q) * 3 + l + r
                            for d in range(3):
                                index = (PAIR_OF[c, d] * 32 + kind) * tile_x + half
                                term = hess_ref[pl.ds(index, 8), :] * fields[3 * m + d]
                                total = term if total is None else total + term
                        value_ref[3 * n + c, rows, :] = total

        def exchange(own, got, sends, receives, index, count, target):
            return [
                remote(
                    own,
                    got.at[k - 1],
                    sends.at[k - 1],
                    receives.at[k - 1],
                    target((index + k) % count),
                )
                for k in range(1, count)
            ]

        def along_x():
            return exchange(own_x, got_x, send_x, recv_x, gx, n_gx, lambda t: (t, gy))

        def along_y():
            return exchange(own_y, got_y, send_y, recv_y, gy, n_gy, lambda t: (gx, t))

        def gather(found, own, got, count):
            for one in found:
                one.wait_recv()
            total = own[...]
            for k in range(1, count):
                total = total + got[k - 1]
            return total

        def inner(left, right):
            total = left[0] * right[0]
            for one, other in zip(left[1:], right[1:]):
                total = total + one * other
            return jnp.sum(total, axis=0, keepdims=True)

        def nothing():
            return None

        def load_part(k):
            start = ((k % 3) * 8 + k // 3) * tile_x
            return load_ref[pl.ds(start, tile_x), :]

        def value_part(k):
            return value_ref[k]

        base = [assemble(0, load_part, nothing)]
        for phase in range(1, ITERS):
            apply()
            base.append(assemble(phase, value_part, nothing))
        apply()
        last = inner([field_ref[k] for k in range(24)], [value_ref[k] for k in range(24)])
        rows = [
            inner(base[0], base[0]),
            inner(base[0], base[1]),
            inner(base[1], base[1]),
            inner(base[1], base[2]),
            inner(base[2], base[2]),
            last,
        ]
        for k in range(6):
            own_x[k : k + 1, :] = rows[k]
        own_x[6:8, :] = jnp.zeros((2, width), jnp.float32)
        for one in along_x():
            one.start()

        def pass_on():
            own_y[...] = gather(along_x(), own_x, got_x, n_gx)
            for one in along_y():
                one.start()

        base.append(assemble(ITERS, value_part, pass_on))
        sums = gather(along_y(), own_y, got_y, n_gy)
        sums = jnp.sum(sums, axis=1, keepdims=True)
        h = [sums[k : k + 1] for k in range(6)]
        sigma = tikhonov / UNIT
        a0 = h[1] / h[0]
        n1 = h[2] - a0 * h[1]
        a1 = (h[3] - 2.0 * a0 * h[2] + a0 * a0 * h[1]) / n1
        s = a0 + a1
        q = a0 * a1 - n1 / h[0]
        n2 = h[4] - s * h[3] + q * h[2]
        a2 = (h[5] - s * h[4] + q * h[3] - s * n2) / n2
        b2 = n2 / n1
        p2 = -(s + a2)
        p1 = q + a2 * s - b2
        p0 = b2 * a0 - a2 * q
        scale = 1.0 / (sigma * (sigma * (p2 - sigma) - p1) + p0)
        r2, r1, r0 = (p2 * scale, p1 * scale, p0 * scale)
        turn_back = -scale / UNIT
        i1 = (p2 - sigma) * turn_back
        i0 = (p1 - sigma * p2 + sigma * sigma) * turn_back
        for a in range(6):
            inc = turn_back * base[2][a] + i1 * base[1][a] + i0 * base[0][a]
            res = scale * base[3][a] + r2 * base[2][a] + r1 * base[1][a] + r0 * base[0][a]
            for out, value in ((inc_ref, inc), (res_ref, res)):
                if a < 3:
                    for layer in range(depth):
                        out[a, layer] = value[:, layer * tile_y : (layer + 1) * tile_y]
                else:
                    out[a - 3, depth] = value[:, width - tile_y :]
        for phase in range(PHASES):
            sent(copies(phase))
        for one in along_x() + along_y():
            one.wait_send()
        sent(y_copies())
        for k in range(BOUND + 1):
            sent([after_copy(k)] + after_corners(k))
        for k in range(BOUND):
            sent([before_copy(k)] + before_corners(k))


def per_device(
    reference_scan, ref_gradient, deformed_scan, interp_weights, sample_mask, block_list, offsets
):
    tile_x, tile_y, column = reference_scan.shape
    depth = column // 512
    width = depth * tile_y
    square_table, shape_table = tables()
    n_gx, n_gy = (lax.axis_size("gx"), lax.axis_size("gy"))
    span_x, span_y = (tile_x + 2 * BOUND + 1, tile_y + 2 * BOUND)
    pos_x = jnp.arange(tile_x)[:, None, None]
    pos_y = jnp.arange(tile_y)[None, :, None]
    layer = jnp.arange(depth)[None, None, :]
    source = (pos_y + offsets[1] + BOUND) * depth + layer
    source = (source * span_x + pos_x + offsets[0] + BOUND) * 4

    def first_pass(s):
        return jnp.minimum(s, tile_x - 1)

    def second_pass(s):
        return row_of(s, tile_x)

    def block(pick):
        return pl.BlockSpec((1, tile_y, column), lambda s: (pick(s), 0, 0))

    def whole(table):
        return pl.BlockSpec(table.shape, lambda s: (0, 0))

    f32, bf16, vmem, dma = (jnp.float32, jnp.bfloat16, pltpu.VMEM, pltpu.SemaphoreType.DMA)
    part = jax.ShapeDtypeStruct((3, depth + 1, tile_x, tile_y), f32)
    result = pl.BlockSpec(part.shape, lambda s: (0, 0, 0, 0))
    halos = 2 + 3 * (2 * BOUND + 1)
    increment, residual = pl.pallas_call(
        functools.partial(step_kernel, (n_gx, n_gy), tile_x, tile_y, depth),
        grid=(2 * tile_x,),
        out_shape=(part, part),
        in_specs=[
            pl.BlockSpec(memory_space=pltpu.SMEM),
            whole(square_table),
            whole(shape_table),
            pl.BlockSpec((3, 1, tile_y, column), lambda s: (0, first_pass(s), 0, 0)),
            block(first_pass),
            block(first_pass),
            block(second_pass),
            block(second_pass),
            pl.BlockSpec(memory_space=pl.ANY),
        ],
        out_specs=(result, result),
        scratch_shapes=[
            vmem((BOUND, tile_y, column), bf16),
            vmem((BOUND + 1, tile_y, column), bf16),
            vmem((span_x, EDGE, column), bf16),
            vmem((span_x, EDGE, column), bf16),
            vmem((span_y * depth * span_x * 4, 128), f32),
            vmem((tile_x, 3, tile_y, column), bf16),
            vmem((6 * width, 512), bf16),
            vmem((width * 8, 128), f32),
            vmem((3 * width, 512), bf16),
            vmem((3 * width, 512), bf16),
            vmem((6 * 32 * tile_x, width), f32),
            vmem((3 * 8 * tile_x, width), f32),
            vmem((24, tile_x, width), f32),
            vmem((24, tile_x, width), f32),
        ]
        + [
            vmem((PHASES, rows, width), f32)
            for rows in (16, 16, tile_x + 8, tile_x + 8) * 2 + (8, 8, 8, 8)
        ]
        + [
            vmem((8, width), f32),
            vmem((n_gx - 1, 8, width), f32),
            vmem((8, width), f32),
            vmem((n_gy - 1, 8, width), f32),
            dma((halos,)),
            dma((halos,)),
            dma((PHASES, 8)),
            dma((PHASES, 8)),
            dma((n_gx - 1,)),
            dma((n_gx - 1,)),
            dma((n_gy - 1,)),
            dma((n_gy - 1,)),
        ],
        compiler_params=pltpu.CompilerParams(collective_id=0, has_side_effects=True),
        name="step",
    )(
        source.reshape(-1),
        jnp.asarray(square_table),
        jnp.asarray(shape_table),
        ref_gradient,
        sample_mask,
        deformed_scan,
        reference_scan,
        interp_weights,
        deformed_scan,
    )

    def nodal(value):
        return jnp.transpose(value, (0, 2, 3, 1))

    return (nodal(increment), nodal(residual))


def solution(mesh):
    return jax.shard_map(
        per_device,
        mesh=mesh,
        in_specs=(
            P("gx", "gy", None),
            P(None, "gx", "gy", None),
            P("gx", "gy", None),
            P("gx", "gy", None),
            P("gx", "gy", None),
            P("gx", "gy"),
            P(None, "gx", "gy", None),
        ),
        out_specs=(P(None, "gx", "gy", None), P(None, "gx", "gy", None)),
        check_vma=False,
    )
```

time: 113 us -> 68.8 us (0.61)
  Pallas kernels: 102 us -> 61.8 us
  other arithmetic: 3.71 us -> 0.61 us
    pallas_call x3 -> x1, Pallas kernels: 102 us -> 61.8 us  [per_device(): pl.pallas_call(functools.partial(step_kernel, (n_gx, n_gy), tile_x, tile_...]
    unnamed x0 -> x2, local copies, waits for them, and re-layouts: none -> 3.12 us
    concatenate x4 -> x0, other arithmetic: 2.66 us -> none  [the longest x2 1.32 us: nodal(): return jnp.concatenate([main, value[3:, :, width - tile_y:, None]], axis=3)]
    broadcast_in_dim x3 -> x0, local copies, waits for them, and re-layouts: 1.62 us -> none  [the longest x2 1.62 us: nodal(): return jnp.concatenate([main, value[3:, :, width - tile_y:, None]], axis=3)]
    slice x5 -> x3, local copies, waits for them, and re-layouts: 2.62 us -> 1.13 us  [the longest x2 0.96 us: per_device(): source = (pos_y + offsets[1] + BOUND) * depth + layer]
where the time goes in v1:
time: 68.8 us; the launch traced here: 68.2 us
  Pallas kernels  61.8 us (90%)
  local copies, waits for them, and re-layouts  5.13 us (7%)
    pallas_call x1, Pallas kernels, per_device(): pl.pallas_call(functools.partial(step_kernel, (n_gx, n_gy), tile_x, tile_...  61.8 us
    unnamed x2, local copies, waits for them, and re-layouts  3.12 us

profile of v1, /device:TPU:0, one launch (start us, length us, event | category | flops | bytes accessed | tf_op | source)
XLA Modules:
  0.0 68.2 jit_solution(17147288218545785280)
XLA Ops:
  0.6 0.8 %fusion = (s32[1,16,32,4]{2,3,1,0:T(4,128)S(1)}, s32[1,16,32,4]{2,3,1,0:T(4,128)S(1)}) fusion(s32[2,16,32,4]{2,3,1,0:T(4,128)} %param.14), kind=kLoop, calls=%fused_computation.1 | loop fusion | bytes 32768 | tf_op jit(solution)/shard_map/slice | solution.py:616
  1.4 0.2 copy.10
  1.6 0.2 squeeze.6
  1.8 0.2 copy.11
  1.9 0.2 squeeze.7
  2.1 0.2 add.53
  2.3 0.2 add.50
  2.5 0.2 add.46
  2.7 0.6 add_multiply_fusion.source_ref
  3.3 61.8 %step.1 = (f32[3,5,16,32]{3,2,1,0:T(8,128)}, f32[3,5,16,32]{3,2,1,0:T(8,128)}) custom-call(s32[2048]{0:T(1024)} %add_multiply_fusion.source_ref, bf16[64,512]{1,0:T(8,128)(2,1)} %constant.8.clone.square_ref, bf16[16,512]{1,0:T(8,128)(2,1)} %constant.9.clone.shape_ref, bf16[3,16,32,2048]{3,2,1,0:T(8,128)(2,1)} %grad_ref.1, s32[16,32,2048]{2,1,0:T(8,128)} %mask_ref.1, ...), custom_call_target="tpu_custom_call" | custom-call | tf_op jit(solution)/shard_map/step/pallas_call | solution.py:635
  65.1 1.6 %copy.14 = f32[3,16,32,5]{2,1,3,0:T(8,128)} copy(f32[3,16,32,5]{2,1,3,0:T(8,128)} %bitcast.7) | data formatting | bytes 61440
  66.7 1.6 %copy.15 = f32[3,16,32,5]{2,1,3,0:T(8,128)} copy(f32[3,16,32,5]{2,1,3,0:T(8,128)} %bitcast.6) | data formatting | bytes 61440
  (3 shorter events, 0.1 us)

commit v2 on v1

v2 whole, which is shorter than its diff:
```python
import functools

import jax
import jax.numpy as jnp
import ml_dtypes
import numpy as np
from jax import lax
from jax.experimental import pallas as pl
from jax.experimental.pallas import tpu as pltpu
from jax.sharding import PartitionSpec as P

BOUND = 4
ITERS = 3
PHASES = ITERS + 1
EDGE = 8

tikhonov = 8.0
UNIT = 64.0

NODES = [(n >> 2 & 1, n >> 1 & 1, n & 1) for n in range(8)]
PAIRS = [(c, d) for c in range(3) for d in range(c, 3)]
PAIR_OF = {(c, d): PAIRS.index((min(c, d), max(c, d))) for c in range(3) for d in range(3)}
MESH = pl.DeviceIdType.MESH


def split(table, count):
    parts = []
    for _ in range(count):
        part = table.astype(ml_dtypes.bfloat16)
        parts.append(part)
        table = table - part.astype(np.float32)
    return parts


def tables():
    voxel = np.arange(512)
    coords = [
        ((voxel // 64).astype(np.float32) + np.float32(0.5)) / np.float32(8.0),
        ((voxel // 8 % 8).astype(np.float32) + np.float32(0.5)) / np.float32(8.0),
        ((voxel % 8).astype(np.float32) + np.float32(0.5)) / np.float32(8.0),
    ]
    linear = [[np.float32(1.0) - t, t] for t in coords]
    quad = [[s[0] * s[0], s[0] * s[1], s[1] * s[1]] for s in linear]
    shapes = np.stack([linear[0][i] * linear[1][j] * linear[2][l] for i, j, l in NODES])
    squares = np.stack(
        [quad[0][a] * quad[1][b] * quad[2][c] for a in range(3) for b in range(3) for c in range(3)]
    )
    squares = np.pad(squares, ((0, 5), (0, 0))) / np.float32(UNIT)
    square_table = np.concatenate(split(squares.astype(np.float32), 2), axis=0)
    shape_table = np.concatenate(split(shapes.astype(np.float32), 2), axis=0)
    return (square_table, shape_table)


def contract(table, part):
    return lax.dot_general(
        table, part, (((1,), (1,)), ((), ())), preferred_element_type=jnp.float32
    )


def row_of(turn, tile_x):
    return jnp.where(turn < tile_x - BOUND, turn + BOUND, tile_x - 1 - turn)


def step_kernel(
    sizes,
    tile_x,
    tile_y,
    depth,
    offset_ref,
    square_ref,
    shape_ref,
    grad_hbm,
    mask_hbm,
    scan_ref,
    image_hbm,
    weight_hbm,
    out_ref,
    grad_ref,
    mask_ref,
    own_ref,
    image_ref,
    weight_ref,
    before_ref,
    after_ref,
    beyond_ref,
    ahead_ref,
    wide_ref,
    part_ref,
    fetched_ref,
    high_ref,
    low_ref,
    hess_ref,
    load_ref,
    field_ref,
    value_ref,
    out_e,
    out_w,
    out_n,
    out_s,
    in_w,
    in_e,
    in_s,
    in_n,
    in_sw,
    in_ne,
    in_nw,
    in_se,
    own_x,
    got_x,
    own_y,
    got_y,
    table_ref,
    source_ref,
    local_sems,
    halo_send,
    halo_recv,
    send_sems,
    recv_sems,
    send_x,
    recv_x,
    send_y,
    recv_y,
):
    n_gx, n_gy = sizes
    gx = lax.axis_index("gx")
    gy = lax.axis_index("gy")
    not_first_x, not_last_x = (gx > 0, gx < n_gx - 1)
    not_first_y, not_last_y = (gy > 0, gy < n_gy - 1)
    both = jnp.logical_and
    wide = depth * tile_y
    span_x = tile_x + 2 * BOUND + 1
    stride_y = depth * span_x * 4

    def remote(source, target, sends, receives, device):
        return pltpu.make_async_remote_copy(
            src_ref=source,
            dst_ref=target,
            send_sem=sends,
            recv_sem=receives,
            device_id=device,
            device_id_type=MESH,
        )

    def halo(k, source, target, device):
        return remote(source, target, halo_send.at[k], halo_recv.at[k], device)

    every = slice(None)
    low_y, high_y = (pl.ds(0, EDGE), pl.ds(tile_y - EDGE, EDGE))
    near_y, far_y = ((gx, gy - 1), (gx, gy + 1))
    middle = pl.ds(BOUND, tile_x)

    def y_copies():
        return [
            (halo(0, scan_ref.at[every, low_y], beyond_ref.at[middle], near_y), not_first_y, not_last_y),
            (halo(1, scan_ref.at[every, high_y], ahead_ref.at[middle], far_y), not_last_y, not_first_y),
        ]

    def after_copy(k):
        return (halo(2 + k, scan_ref.at[k], after_ref.at[k], (gx - 1, gy)), not_first_x, not_last_x)

    def before_copy(k):
        source = scan_ref.at[tile_x - BOUND + k]
        return (
            halo(3 + BOUND + k, source, before_ref.at[k], (gx + 1, gy)),
            not_last_x,
            not_first_x,
        )

    def corner_copies(first, band, k, row, present):
        return [
            (
                halo(first, band.at[k, low_y], beyond_ref.at[row], near_y),
                both(present, not_first_y),
                both(present, not_last_y),
            ),
            (
                halo(first + 1, band.at[k, high_y], ahead_ref.at[row], far_y),
                both(present, not_last_y),
                both(present, not_first_y),
            ),
        ]

    def after_corners(k):
        first = 3 + 2 * BOUND + 2 * k
        return corner_copies(first, after_ref, k, BOUND + tile_x + k, not_last_x)

    def before_corners(k):
        first = 5 + 4 * BOUND + 2 * k
        return corner_copies(first, before_ref, k, k, not_first_x)

    def begin(copies):
        for one, sends, _ in copies:
            pl.when(sends)(one.start)

    def arrive(copies):
        for one, _, receives in copies:
            pl.when(receives)(one.wait_recv)

    def sent(copies):
        for one, sends, _ in copies:
            pl.when(sends)(one.wait_send)

    def put_wide(value, at_x, at_y):
        count = value.shape[0]
        for layer in range(depth):
            for chunk in range(4):
                lanes = slice(layer * 512 + chunk * 128, layer * 512 + chunk * 128 + 128)
                start = at_y * stride_y + (layer * span_x + at_x) * 4 + chunk
                wide_ref[pl.ds(start, count, stride=stride_y), :] = value[:, lanes]

    def put_sides(row, inside):
        value = beyond_ref[row].astype(jnp.float32)[0:BOUND]
        put_wide(jnp.where(both(inside, not_last_y), value, 0.0), row, BOUND + tile_y)
        value = ahead_ref[row].astype(jnp.float32)[EDGE - BOUND :]
        put_wide(jnp.where(both(inside, not_first_y), value, 0.0), row, 0)

    def put_band(band, k, row, inside):
        for first in range(0, tile_y, 16):
            value = band[k, pl.ds(first, 16), :].astype(jnp.float32)
            put_wide(jnp.where(inside, value, 0.0), row, BOUND + first)
        put_sides(row, inside)

    def first_copies(x):
        return [
            pltpu.make_async_copy(grad_hbm.at[:, x], grad_ref.at[:, x], local_sems.at[0, x]),
            pltpu.make_async_copy(mask_hbm.at[x], mask_ref.at[x], local_sems.at[1, x]),
            pltpu.make_async_copy(scan_ref.at[x], own_ref.at[x], local_sems.at[2, x]),
        ]

    def second_copies(x):
        return [
            pltpu.make_async_copy(image_hbm.at[x], image_ref.at[x], local_sems.at[3, x]),
            pltpu.make_async_copy(weight_hbm.at[x], weight_ref.at[x], local_sems.at[4, x]),
        ]

    def start_first(x, carry):
        for one in first_copies(x):
            one.start()
        return carry

    def start_second(turn, carry):
        for one in second_copies(row_of(turn, tile_x)):
            one.start()
        return carry

    for buffer in (in_w, in_e, in_s, in_n, in_sw, in_ne, in_nw, in_se):
        buffer[...] = jnp.zeros_like(buffer)
    for buffer in (out_e, out_w, out_n, out_s):
        buffer[...] = jnp.zeros_like(buffer)
    barrier = pltpu.get_barrier_semaphore()
    for k in range(1, n_gx):
        pl.semaphore_signal(
            barrier, inc=1, device_id=((gx + k) % n_gx, gy), device_id_type=MESH
        )
    for k in range(1, n_gy):
        pl.semaphore_signal(
            barrier, inc=1, device_id=(gx, (gy + k) % n_gy), device_id_type=MESH
        )
    corners = 0
    for dx, there_x in ((-1, not_first_x), (1, not_last_x)):
        for dy, there_y in ((-1, not_first_y), (1, not_last_y)):
            present = both(there_x, there_y)
            corners = corners + jnp.where(present, 1, 0)

            @pl.when(present)
            def _(dx=dx, dy=dy):
                pl.semaphore_signal(
                    barrier, inc=1, device_id=(gx + dx, gy + dy), device_id_type=MESH
                )

    lax.fori_loop(0, tile_x, start_first, 0)
    extent = (tile_x, depth, tile_y)
    pos_x, layers, pos_y = [lax.broadcasted_iota(jnp.int32, extent, k) for k in range(3)]
    table = (pos_y + offset_ref[1] + BOUND) * depth + layers
    table_ref[...] = (table * span_x + pos_x + offset_ref[0] + BOUND) * 4
    table_copy = pltpu.make_async_copy(table_ref, source_ref, local_sems.at[5, 0])
    table_copy.start()
    pl.semaphore_wait(barrier, n_gx - 1 + n_gy - 1 + corners)
    begin(y_copies())
    begin([after_copy(k) for k in range(BOUND + 1)])
    begin([before_copy(BOUND - 1 - k) for k in range(BOUND)])
    lax.fori_loop(0, tile_x, start_second, 0)

    def hessian_row(x, carry):
        for one in first_copies(x):
            one.wait()
        for first in range(0, tile_y, 16):
            value = own_ref[x, pl.ds(first, 16), :].astype(jnp.float32)
            put_wide(value, BOUND + x, BOUND + first)
        for layer in range(depth):
            lanes = pl.ds(layer * 512, 512)
            mask = mask_ref[x, :, lanes].astype(jnp.float32).astype(jnp.bfloat16)
            grads = [grad_ref[c, x, :, lanes] for c in range(3)]
            masked = [mask * g for g in grads]
            for c in range(3):
                grad_ref[c, x, :, lanes] = masked[c]
            for q, (c, d) in enumerate(PAIRS):
                part_ref[pl.ds(q * wide + layer * tile_y, tile_y), :] = masked[c] * grads[d]
        table = square_ref[...]
        for q in range(6):
            total = contract(table, part_ref[pl.ds(q * wide, wide), :])
            value = total[0:32] + total[32:64]
            for first in range(0, 32, 8):
                rows = pl.ds((q * 32 + first) * tile_x + x, 8, stride=tile_x)
                hess_ref[rows, :] = value[first : first + 8]
        return carry

    lax.fori_loop(0, tile_x, hessian_row, 0)
    table_copy.wait()
    arrive(y_copies())

    def convert(i, carry):
        put_sides(BOUND + i, gx >= 0)
        return carry

    lax.fori_loop(0, tile_x, convert, 0)
    head = tile_x - 2 * BOUND - 1
    turned = tile_x - BOUND

    def load_row(turn, carry):
        @pl.when(both(turn >= head - 2, turn < turned - 2))
        def _():
            k = turn - (head - 2)
            arrive([after_copy(k)])
            begin(after_corners(k))

        @pl.when(both(turn >= turned - 2, turn < tile_x - 2))
        def _():
            k = tile_x - 3 - turn
            arrive([before_copy(k)])
            begin(before_corners(k))

        @pl.when(both(turn >= head, turn < turned))
        def _():
            k = turn - head
            arrive(after_corners(k))
            put_band(after_ref, k, BOUND + tile_x + k, not_last_x)

        @pl.when(turn >= turned)
        def _():
            k = tile_x - 1 - turn
            arrive(before_corners(k))
            put_band(before_ref, k, k, not_first_x)

        x = row_of(turn, tile_x)
        for one in second_copies(x):
            one.wait()

        def fetch(block, inner_carry):
            for inner in range(4):
                y = block * 4 + inner
                for layer in range(depth):
                    row = source_ref[x, layer, y]
                    rows = pl.ds(pl.multiple_of((y * depth + layer) * 8, 8), 8)
                    fetched_ref[rows, :] = wide_ref[pl.ds(row, 8), :]
            return inner_carry

        lax.fori_loop(0, tile_y // 4, fetch, 0)
        for layer in range(depth):
            for chunk in range(4):
                lanes = pl.ds(layer * 512 + chunk * 128, 128)
                part = pl.ds(chunk * 128, 128)
                near = fetched_ref[pl.ds(layer * 8 + chunk, tile_y, stride=8 * depth), :]
                far = fetched_ref[pl.ds(layer * 8 + 4 + chunk, tile_y, stride=8 * depth), :]
                weight = weight_ref[x, :, lanes].astype(jnp.float32)
                warped = weight * near + (1.0 - weight) * far
                image = image_ref[x, :, lanes].astype(jnp.float32) - warped
                image = image.astype(jnp.bfloat16).astype(jnp.float32)
                for c in range(3):
                    rows = pl.ds(c * wide + layer * tile_y, tile_y)
                    value = image * grad_ref[c, x, :, lanes].astype(jnp.float32)
                    high = value.astype(jnp.bfloat16)
                    high_ref[rows, part] = high
                    low_ref[rows, part] = (value - high.astype(jnp.float32)).astype(jnp.bfloat16)
        table = shape_ref[...]
        for c in range(3):
            rows = pl.ds(c * wide, wide)
            total = contract(table, high_ref[rows, :]) + contract(table, low_ref[rows, :])
            load_ref[pl.ds(c * 8 * tile_x + x, 8, stride=tile_x), :] = total[0:8] + total[8:16]
        return carry

    lax.fori_loop(0, tile_x, load_row, 0)

    width = wide
    lane = lax.broadcasted_iota(jnp.int32, (tile_x, width), 1)
    row = lax.broadcasted_iota(jnp.int32, (tile_x, width), 0)
    in_tile = lane % tile_y
    first_y = in_tile == 0
    last_y = in_tile == tile_y - 1
    first_x = row == 0
    last_x = row == tile_x - 1
    topmost = lane >= width - tile_y
    above = lane >= tile_y
    first_8, last_8 = (first_y[0:8], last_y[0:8])
    turn_y = tile_y - 1
    body, tail = (pl.ds(0, tile_x), pl.ds(tile_x, 8))
    upper, lower = (pl.ds(0, 8), pl.ds(8, 8))

    def roll(value, shift, axis):
        return pltpu.roll(value, shift % value.shape[axis], axis)

    def shift_x(value):
        return jnp.where(first_x, 0.0, roll(value, 1, 0))

    def copies(phase):
        table = [
            (out_e, None, in_w, 1, 0),
            (out_n, None, in_s, 0, 1),
            (out_e, lower, in_sw, 1, 1),
            (out_w, None, in_e, -1, 0),
            (out_s, None, in_n, 0, -1),
            (out_w, upper, in_ne, -1, -1),
            (out_e, upper, in_nw, 1, -1),
            (out_w, lower, in_se, -1, 1),
        ]
        if phase == PHASES - 1:
            table = table[:3]
        found = []
        for k, (src, rows, dst, dx, dy) in enumerate(table):
            send_ok, recv_ok = (gx >= 0, gx >= 0)
            if dx:
                send_ok = not_last_x if dx > 0 else not_first_x
                recv_ok = not_first_x if dx > 0 else not_last_x
            if dy:
                send_ok = both(send_ok, not_last_y if dy > 0 else not_first_y)
                recv_ok = both(recv_ok, not_first_y if dy > 0 else not_last_y)
            source = src.at[phase] if rows is None else src.at[phase, rows]
            one = remote(
                source,
                dst.at[phase],
                send_sems.at[phase, k],
                recv_sems.at[phase, k],
                (gx + dx, gy + dy),
            )
            found.append((one, send_ok, recv_ok))
        return found

    def assemble(phase, partial, meanwhile):
        folded = {}
        for i in range(2):
            for j in range(2):
                found = []
                for c in range(3):
                    under = partial((4 * i + 2 * j) * 3 + c)
                    over = partial((4 * i + 2 * j + 1) * 3 + c)
                    found.append(under + jnp.where(above, roll(over, tile_y, 1), 0.0))
                    folded[i, j, 3 + c] = jnp.where(topmost, over, 0.0)
                for c in range(3):
                    folded[i, j, c] = found[c]
        total, right = ([], [])
        north = jnp.zeros((tile_x, width), jnp.float32)
        south = jnp.zeros((tile_x, width), jnp.float32)
        for a in range(6):
            kept = [
                folded[i, 0, a] + jnp.where(first_y, 0.0, roll(folded[i, 1, a], 1, 1))
                for i in range(2)
            ]
            mine = kept[0] + shift_x(kept[1])
            side = folded[0, 1, a] + shift_x(folded[1, 1, a])
            edge_x = kept[1][tile_x - 1 :]
            edge_c = folded[1, 1, a][tile_x - 1 :]
            out_e[phase, a : a + 1, :] = edge_x
            out_e[phase, 8 + a : 9 + a, :] = edge_c
            out_w[phase, a : a + 1, :] = mine[0:1]
            out_w[phase, 8 + a : 9 + a, :] = side[0:1]
            out_n[phase, tile_x + a : tile_x + a + 1, :] = edge_c
            out_s[phase, tile_x + a : tile_x + a + 1, :] = edge_x
            north = jnp.where(in_tile == a, roll(side, a + 1, 1), north)
            south = jnp.where(in_tile == a, roll(mine, a, 1), south)
            total.append(mine)
            right.append(side)
        out_n[phase, body, :] = north
        out_s[phase, body, :] = south
        begin(copies(phase))
        meanwhile()
        arrive(copies(phase))
        line = in_w[phase, upper, :] + jnp.where(
            first_8, roll(in_sw[phase], -turn_y, 1), 0.0
        )
        from_s = in_s[phase, body, :]
        whole = [
            total[a]
            + jnp.where(first_x, line[a : a + 1], 0.0)
            + jnp.where(first_y, roll(from_s, -(tile_y + a), 1), 0.0)
            for a in range(6)
        ]
        if phase == PHASES - 1:
            return whole
        side_x = in_s[phase, tail, :] + in_se[phase]
        side_x = jnp.where(first_8, roll(side_x, -turn_y, 1), 0.0)
        side_x = jnp.where(not_last_x, out_e[phase, upper, :] + in_e[phase, upper, :] + side_x, 0.0)
        line = in_w[phase, lower, :] + roll(in_nw[phase], turn_y, 1)
        corner = in_n[phase, tail, :] + in_ne[phase]
        corner = out_e[phase, lower, :] + in_e[phase, lower, :] + roll(corner, turn_y, 1)
        corner = jnp.where(both(not_last_x, not_last_y), corner, 0.0)
        corner = jnp.where(last_8, corner, roll(side_x, -1, 1))
        from_n = in_n[phase, body, :]
        for a in range(6):
            side = right[a] + jnp.where(first_x, line[a : a + 1], 0.0)
            side = side + roll(from_n, turn_y - a, 1)
            side = jnp.where(not_last_y, side, 0.0)
            next_x = jnp.where(last_x, side_x[a : a + 1], roll(whole[a], -1, 0))
            next_y = jnp.where(last_y, side, roll(whole[a], -1, 1))
            next_c = jnp.where(last_x, corner[a : a + 1], roll(next_y, -1, 0))
            for k, value in enumerate((whole[a], next_y, next_x, next_c)):
                if a < 3:
                    field_ref[6 * k + a] = value
                    field_ref[6 * k + 3 + a] = roll(value, -tile_y, 1)
                else:
                    above_it = field_ref[6 * k + a]
                    field_ref[6 * k + a] = jnp.where(topmost, value, above_it)
        return whole

    def apply():
        for half in range(0, tile_x, 8):
            rows = pl.ds(half, 8)
            fields = [field_ref[k, rows, :] for k in range(24)]
            for n, (i, j, l) in enumerate(NODES):
                for c in range(3):
                    total = None
                    for m, (p, q, r) in enumerate(NODES):
                        kind = (i + p) * 9 + (j + q) * 3 + l + r
                        for d in range(3):
                            index = (PAIR_OF[c, d] * 32 + kind) * tile_x + half
                            term = hess_ref[pl.ds(index, 8), :] * fields[3 * m + d]
                            total = term if total is None else total + term
                    value_ref[3 * n + c, rows, :] = total

    def exchange(own, got, sends, receives, index, count, target):
        return [
            remote(
                own,
                got.at[k - 1],
                sends.at[k - 1],
                receives.at[k - 1],
                target((index + k) % count),
            )
            for k in range(1, count)
        ]

    def along_x():
        return exchange(own_x, got_x, send_x, recv_x, gx, n_gx, lambda t: (t, gy))

    def along_y():
        return exchange(own_y, got_y, send_y, recv_y, gy, n_gy, lambda t: (gx, t))

    def gather(found, own, got, count):
        for one in found:
            one.wait_recv()
        total = own[...]
        for k in range(1, count):
            total = total + got[k - 1]
        return total

    def inner(left, right):
        total = left[0] * right[0]
        for one, other in zip(left[1:], right[1:]):
            total = total + one * other
        return jnp.sum(total, axis=0, keepdims=True)

    def nothing():
        return None

    def load_part(k):
        start = ((k % 3) * 8 + k // 3) * tile_x
        return load_ref[pl.ds(start, tile_x), :]

    def value_part(k):
        return value_ref[k]

    base = [assemble(0, load_part, nothing)]
    for phase in range(1, ITERS):
        apply()
        base.append(assemble(phase, value_part, nothing))
    apply()
    last = inner([field_ref[k] for k in range(24)], [value_ref[k] for k in range(24)])
    rows = [
        inner(base[0], base[0]),
        inner(base[0], base[1]),
        inner(base[1], base[1]),
        inner(base[1], base[2]),
        inner(base[2], base[2]),
        last,
    ]
    for k in range(6):
        own_x[k : k + 1, :] = rows[k]
    own_x[6:8, :] = jnp.zeros((2, width), jnp.float32)
    for one in along_x():
        one.start()

    def pass_on():
        own_y[...] = gather(along_x(), own_x, got_x, n_gx)
        for one in along_y():
            one.start()

    base.append(assemble(ITERS, value_part, pass_on))
    sums = gather(along_y(), own_y, got_y, n_gy)
    sums = jnp.sum(sums, axis=1, keepdims=True)
    h = [sums[k : k + 1] for k in range(6)]
    sigma = tikhonov / UNIT
    a0 = h[1] / h[0]
    n1 = h[2] - a0 * h[1]
    a1 = (h[3] - 2.0 * a0 * h[2] + a0 * a0 * h[1]) / n1
    s = a0 + a1
    q = a0 * a1 - n1 / h[0]
    n2 = h[4] - s * h[3] + q * h[2]
    a2 = (h[5] - s * h[4] + q * h[3] - s * n2) / n2
    b2 = n2 / n1
    p2 = -(s + a2)
    p1 = q + a2 * s - b2
    p0 = b2 * a0 - a2 * q
    scale = 1.0 / (sigma * (sigma * (p2 - sigma) - p1) + p0)
    r2, r1, r0 = (p2 * scale, p1 * scale, p0 * scale)
    turn_back = -scale / UNIT
    i1 = (p2 - sigma) * turn_back
    i0 = (p1 - sigma * p2 + sigma * sigma) * turn_back
    for a in range(6):
        inc = turn_back * base[2][a] + i1 * base[1][a] + i0 * base[0][a]
        res = scale * base[3][a] + r2 * base[2][a] + r1 * base[1][a] + r0 * base[0][a]
        out_ref[a] = inc
        out_ref[6 + a] = res
    for phase in range(PHASES):
        sent(copies(phase))
    for one in along_x() + along_y():
        one.wait_send()
    sent(y_copies())
    for k in range(BOUND + 1):
        sent([after_copy(k)] + after_corners(k))
    for k in range(BOUND):
        sent([before_copy(k)] + before_corners(k))


def format_kernel(depth, value_ref, inc_ref, res_ref):
    tile_y = inc_ref.shape[3]
    width = value_ref.shape[2]
    for out, first in ((inc_ref, 0), (res_ref, 6)):
        for c in range(3):
            value = value_ref[first + c]
            for layer in range(depth):
                out[c, layer] = value[:, layer * tile_y : (layer + 1) * tile_y]
            out[c, depth] = value_ref[first + 3 + c][:, width - tile_y :]


def per_device(
    reference_scan, ref_gradient, deformed_scan, interp_weights, sample_mask, block_list, offsets
):
    tile_x, tile_y, column = reference_scan.shape
    depth = column // 512
    width = depth * tile_y
    square_table, shape_table = tables()
    n_gx, n_gy = (lax.axis_size("gx"), lax.axis_size("gy"))
    span_x, span_y = (tile_x + 2 * BOUND + 1, tile_y + 2 * BOUND)
    f32, bf16, vmem, dma = (jnp.float32, jnp.bfloat16, pltpu.VMEM, pltpu.SemaphoreType.DMA)
    part = jax.ShapeDtypeStruct((3, depth + 1, tile_x, tile_y), f32)
    halos = 2 + 3 * (2 * BOUND + 1)
    whole = pl.BlockSpec(memory_space=pltpu.VMEM)
    anywhere = pl.BlockSpec(memory_space=pl.ANY)
    packed = pl.pallas_call(
        functools.partial(step_kernel, (n_gx, n_gy), tile_x, tile_y, depth),
        out_shape=jax.ShapeDtypeStruct((12, tile_x, width), f32),
        in_specs=[whole] * 3 + [anywhere] * 5,
        out_specs=whole,
        scratch_shapes=[
            vmem((3, tile_x, tile_y, column), bf16),
            vmem((tile_x, tile_y, column), jnp.int32),
            vmem((tile_x, tile_y, column), bf16),
            vmem((tile_x, tile_y, column), bf16),
            vmem((tile_x, tile_y, column), bf16),
            vmem((BOUND, tile_y, column), bf16),
            vmem((BOUND + 1, tile_y, column), bf16),
            vmem((span_x, EDGE, column), bf16),
            vmem((span_x, EDGE, column), bf16),
            vmem((span_y * depth * span_x * 4, 128), f32),
            vmem((6 * width, 512), bf16),
            vmem((width * 8, 128), f32),
            vmem((3 * width, 512), bf16),
            vmem((3 * width, 512), bf16),
            vmem((6 * 32 * tile_x, width), f32),
            vmem((3 * 8 * tile_x, width), f32),
            vmem((24, tile_x, width), f32),
            vmem((24, tile_x, width), f32),
        ]
        + [
            vmem((PHASES, rows, width), f32)
            for rows in (16, 16, tile_x + 8, tile_x + 8) * 2 + (8, 8, 8, 8)
        ]
        + [
            vmem((8, width), f32),
            vmem((n_gx - 1, 8, width), f32),
            vmem((8, width), f32),
            vmem((n_gy - 1, 8, width), f32),
            vmem((tile_x, depth, tile_y), jnp.int32),
            pltpu.SMEM((tile_x, depth, tile_y), jnp.int32),
            dma((6, tile_x)),
            dma((halos,)),
            dma((halos,)),
            dma((PHASES, 8)),
            dma((PHASES, 8)),
            dma((n_gx - 1,)),
            dma((n_gx - 1,)),
            dma((n_gy - 1,)),
            dma((n_gy - 1,)),
        ],
        compiler_params=pltpu.CompilerParams(collective_id=0, has_side_effects=True),
        name="step",
    )(
        jnp.transpose(offsets, (0, 1, 3, 2)),
        jnp.asarray(square_table),
        jnp.asarray(shape_table),
        ref_gradient,
        sample_mask,
        deformed_scan,
        reference_scan,
        interp_weights,
    )
    increment, residual = pl.pallas_call(
        functools.partial(format_kernel, depth),
        out_shape=(part, part),
        in_specs=[whole],
        out_specs=(whole, whole),
        name="format",
    )(packed)

    def nodal(value):
        return jnp.transpose(value, (0, 2, 3, 1))

    return (nodal(increment), nodal(residual))


def solution(mesh):
    return jax.shard_map(
        per_device,
        mesh=mesh,
        in_specs=(
            P("gx", "gy", None),
            P(None, "gx", "gy", None),
            P("gx", "gy", None),
            P("gx", "gy", None),
            P("gx", "gy", None),
            P("gx", "gy"),
            P(None, "gx", "gy", None),
        ),
        out_specs=(P(None, "gx", "gy", None), P(None, "gx", "gy", None)),
        check_vma=False,
    )
```

time: 68.8 us -> 64.7 us (0.940)
  local copies, waits for them, and re-layouts: 5.13 us -> 0 us
  Pallas kernels: 61.8 us -> 63.9 us
    unnamed x2 -> x0, local copies, waits for them, and re-layouts: 3.12 us -> none
    pallas_call x0 -> x1, Pallas kernels: none -> 1.67 us  [per_device(): pl.pallas_call(functools.partial(format_kernel, depth), out_shape=(part,...]
    slice x3 -> x0, local copies, waits for them, and re-layouts: 1.13 us -> none  [the longest x2 0.96 us: per_device(): source = (pos_y + offsets[1] + BOUND) * depth + layer]
where the time goes in v2:
time: 64.7 us; the launch traced here: 64.6 us
  Pallas kernels  63.9 us (99%)
    pallas_call x1, Pallas kernels, per_device(): pl.pallas_call(functools.partial(step_kernel, (n_gx, n_gy), tile_x, tile_...  62.2 us
    pallas_call x1, Pallas kernels, per_device(): pl.pallas_call(functools.partial(format_kernel, depth), out_shape=(part,...  1.67 us

profile of v2, /device:TPU:0, one launch (start us, length us, event | category | flops | bytes accessed | tf_op | source)
XLA Modules:
  0.0 64.6 jit_solution(18105438941106988019)
XLA Ops:
  0.6 62.2 %step.1.value_ref = f32[12,16,128]{2,1,0:T(8,128)} custom-call(s32[2,16,4,32]{3,2,1,0:T(4,128)} %bitcast.3, bf16[64,512]{1,0:T(8,128)(2,1)} %constant.4.clone.square_ref, bf16[16,512]{1,0:T(8,128)(2,1)} %constant.5.clone.shape_ref, bf16[3,16,32,2048]{3,2,1,0:T(8,128)(2,1)} %grad_hbm.1, s32[16,32,2048]{2,1,0:T(8,128)} %mask_hbm.1, ...), custom_call_target="tpu_custom_call" | custom-call | tf_op jit(solution)/shard_map/step/pallas_call | solution.py:658
  62.9 1.7 %format.1 = (f32[3,5,16,32]{3,2,1,0:T(8,128)}, f32[3,5,16,32]{3,2,1,0:T(8,128)}) custom-call(f32[12,16,128]{2,1,0:T(8,128)} %step.1.value_ref), custom_call_target="tpu_custom_call" | custom-call | tf_op jit(solution)/shard_map/format/pallas_call | solution.py:716

commit v3 on v2

--- a/solution.py
+++ b/solution.py
@@ -49,6 +49,10 @@
     square_table = np.concatenate(split(squares.astype(np.float32), 2), axis=0)
     shape_table = np.concatenate(split(shapes.astype(np.float32), 2), axis=0)
     return (square_table, shape_table)
+
+
+def spread_stride(rows):
+    return rows + 4 if rows % 8 == 0 else rows
 
 
 def contract(table, part):
@@ -129,7 +133,9 @@
     both = jnp.logical_and
     wide = depth * tile_y
     span_x = tile_x + 2 * BOUND + 1
-    stride_y = depth * span_x * 4
+    stride_y = spread_stride(depth * span_x * 4)
+    stride_x = spread_stride(tile_x)
+    stride_f = spread_stride(8 * depth)
 
     def remote(source, target, sends, receives, device):
         return pltpu.make_async_remote_copy(
@@ -155,16 +161,34 @@
             (halo(1, scan_ref.at[every, high_y], ahead_ref.at[middle], far_y), not_last_y, not_first_y),
         ]
 
-    def after_copy(k):
-        return (halo(2 + k, scan_ref.at[k], after_ref.at[k], (gx - 1, gy)), not_first_x, not_last_x)
-
-    def before_copy(k):
-        source = scan_ref.at[tile_x - BOUND + k]
-        return (
-            halo(3 + BOUND + k, source, before_ref.at[k], (gx + 1, gy)),
-            not_last_x,
-            not_first_x,
-        )
+    inner_y = pl.ds(EDGE, tile_y - 2 * EDGE)
+    bands = 2 * BOUND + 1
+
+    def after_parts(k, parts):
+        return [
+            (
+                halo(2 + 3 * k + p, scan_ref.at[k, cut], after_ref.at[k, cut], (gx - 1, gy)),
+                not_first_x,
+                not_last_x,
+            )
+            for p, cut in enumerate((low_y, high_y, inner_y))
+            if p in parts
+        ]
+
+    def before_parts(k, parts):
+        row = tile_x - BOUND + k
+        first = 5 + 3 * BOUND + 3 * k
+        return [
+            (
+                halo(first + p, scan_ref.at[row, cut], before_ref.at[k, cut], (gx + 1, gy)),
+                not_last_x,
+                not_first_x,
+            )
+            for p, cut in enumerate((low_y, high_y, inner_y))
+            if p in parts
+        ]
+
+    edges, rest, whole_row = ((0, 1), (2,), (0, 1, 2))
 
     def corner_copies(first, band, k, row, present):
         return [
@@ -181,11 +205,11 @@
         ]
 
     def after_corners(k):
-        first = 3 + 2 * BOUND + 2 * k
+        first = 2 + 3 * bands + 2 * k
         return corner_copies(first, after_ref, k, BOUND + tile_x + k, not_last_x)
 
     def before_corners(k):
-        first = 5 + 4 * BOUND + 2 * k
+        first = 4 + 3 * bands + 2 * BOUND + 2 * k
         return corner_copies(first, before_ref, k, k, not_first_x)
 
     def begin(copies):
@@ -268,17 +292,21 @@
                     barrier, inc=1, device_id=(gx + dx, gy + dy), device_id_type=MESH
                 )
 
-    lax.fori_loop(0, tile_x, start_first, 0)
+    lax.fori_loop(0, 2, start_first, 0)
     extent = (tile_x, depth, tile_y)
     pos_x, layers, pos_y = [lax.broadcasted_iota(jnp.int32, extent, k) for k in range(3)]
-    table = (pos_y + offset_ref[1] + BOUND) * depth + layers
-    table_ref[...] = (table * span_x + pos_x + offset_ref[0] + BOUND) * 4
+    table = (pos_y + offset_ref[1] + BOUND) * stride_y
+    table_ref[...] = table + (layers * span_x + pos_x + offset_ref[0] + BOUND) * 4
     table_copy = pltpu.make_async_copy(table_ref, source_ref, local_sems.at[5, 0])
     table_copy.start()
     pl.semaphore_wait(barrier, n_gx - 1 + n_gy - 1 + corners)
     begin(y_copies())
-    begin([after_copy(k) for k in range(BOUND + 1)])
-    begin([before_copy(BOUND - 1 - k) for k in range(BOUND)])
+    for parts in (edges, rest):
+        for k in range(BOUND + 1):
+            begin(after_parts(k, parts))
+        for k in range(BOUND):
+            begin(before_parts(BOUND - 1 - k, parts))
+    lax.fori_loop(2, tile_x, start_first, 0)
     lax.fori_loop(0, tile_x, start_second, 0)
 
     def hessian_row(x, carry):
@@ -301,7 +329,7 @@
             total = contract(table, part_ref[pl.ds(q * wide, wide), :])
             value = total[0:32] + total[32:64]
             for first in range(0, 32, 8):
-                rows = pl.ds((q * 32 + first) * tile_x + x, 8, stride=tile_x)
+                rows = pl.ds((q * 32 + first) * stride_x + x, 8, stride=stride_x)
                 hess_ref[rows, :] = value[first : first + 8]
         return carry
 
@@ -318,28 +346,28 @@
     turned = tile_x - BOUND
 
     def load_row(turn, carry):
-        @pl.when(both(turn >= head - 2, turn < turned - 2))
+        @pl.when(both(turn >= head - BOUND - 1, turn < head))
         def _():
-            k = turn - (head - 2)
-            arrive([after_copy(k)])
+            k = turn - (head - BOUND - 1)
+            arrive(after_parts(k, edges))
             begin(after_corners(k))
 
-        @pl.when(both(turn >= turned - 2, turn < tile_x - 2))
+        @pl.when(both(turn >= head - BOUND, turn < head))
         def _():
-            k = tile_x - 3 - turn
-            arrive([before_copy(k)])
+            k = head - 1 - turn
+            arrive(before_parts(k, edges))
             begin(before_corners(k))
 
         @pl.when(both(turn >= head, turn < turned))
         def _():
             k = turn - head
-            arrive(after_corners(k))
+            arrive(after_parts(k, rest) + after_corners(k))
             put_band(after_ref, k, BOUND + tile_x + k, not_last_x)
 
         @pl.when(turn >= turned)
         def _():
             k = tile_x - 1 - turn
-            arrive(before_corners(k))
+            arrive(before_parts(k, rest) + before_corners(k))
             put_band(before_ref, k, k, not_first_x)
 
         x = row_of(turn, tile_x)
@@ -351,7 +379,7 @@
                 y = block * 4 + inner
                 for layer in range(depth):
                     row = source_ref[x, layer, y]
-                    rows = pl.ds(pl.multiple_of((y * depth + layer) * 8, 8), 8)
+                    rows = pl.ds(y * stride_f + layer * 8, 8)
                     fetched_ref[rows, :] = wide_ref[pl.ds(row, 8), :]
             return inner_carry
 
@@ -360,8 +388,8 @@
             for chunk in range(4):
                 lanes = pl.ds(layer * 512 + chunk * 128, 128)
                 part = pl.ds(chunk * 128, 128)
-                near = fetched_ref[pl.ds(layer * 8 + chunk, tile_y, stride=8 * depth), :]
-                far = fetched_ref[pl.ds(layer * 8 + 4 + chunk, tile_y, stride=8 * depth), :]
+                near = fetched_ref[pl.ds(layer * 8 + chunk, tile_y, stride=stride_f), :]
+                far = fetched_ref[pl.ds(layer * 8 + 4 + chunk, tile_y, stride=stride_f), :]
                 weight = weight_ref[x, :, lanes].astype(jnp.float32)
                 warped = weight * near + (1.0 - weight) * far
                 image = image_ref[x, :, lanes].astype(jnp.float32) - warped
@@ -376,7 +404,7 @@
         for c in range(3):
             rows = pl.ds(c * wide, wide)
             total = contract(table, high_ref[rows, :]) + contract(table, low_ref[rows, :])
-            load_ref[pl.ds(c * 8 * tile_x + x, 8, stride=tile_x), :] = total[0:8] + total[8:16]
+            load_ref[pl.ds(c * 8 * stride_x + x, 8, stride=stride_x), :] = total[0:8] + total[8:16]
         return carry
 
     lax.fori_loop(0, tile_x, load_row, 0)
@@ -521,7 +549,7 @@
                     for m, (p, q, r) in enumerate(NODES):
                         kind = (i + p) * 9 + (j + q) * 3 + l + r
                         for d in range(3):
-                            index = (PAIR_OF[c, d] * 32 + kind) * tile_x + half
+                            index = (PAIR_OF[c, d] * 32 + kind) * stride_x + half
                             term = hess_ref[pl.ds(index, 8), :] * fields[3 * m + d]
                             total = term if total is None else total + term
                     value_ref[3 * n + c, rows, :] = total
@@ -562,7 +590,7 @@
         return None
 
     def load_part(k):
-        start = ((k % 3) * 8 + k // 3) * tile_x
+        start = ((k % 3) * 8 + k // 3) * stride_x
         return load_ref[pl.ds(start, tile_x), :]
 
     def value_part(k):
@@ -625,9 +653,9 @@
         one.wait_send()
     sent(y_copies())
     for k in range(BOUND + 1):
-        sent([after_copy(k)] + after_corners(k))
+        sent(after_parts(k, whole_row) + after_corners(k))
     for k in range(BOUND):
-        sent([before_copy(k)] + before_corners(k))
+        sent(before_parts(k, whole_row) + before_corners(k))
 
 
 def format_kernel(depth, value_ref, inc_ref, res_ref):
@@ -652,7 +680,7 @@
     span_x, span_y = (tile_x + 2 * BOUND + 1, tile_y + 2 * BOUND)
     f32, bf16, vmem, dma = (jnp.float32, jnp.bfloat16, pltpu.VMEM, pltpu.SemaphoreType.DMA)
     part = jax.ShapeDtypeStruct((3, depth + 1, tile_x, tile_y), f32)
-    halos = 2 + 3 * (2 * BOUND + 1)
+    halos = 2 + 5 * (2 * BOUND + 1)
     whole = pl.BlockSpec(memory_space=pltpu.VMEM)
     anywhere = pl.BlockSpec(memory_space=pl.ANY)
     packed = pl.pallas_call(
@@ -670,13 +698,13 @@
             vmem((BOUND + 1, tile_y, column), bf16),
             vmem((span_x, EDGE, column), bf16),
             vmem((span_x, EDGE, column), bf16),
-            vmem((span_y * depth * span_x * 4, 128), f32),
+            vmem((span_y * spread_stride(depth * span_x * 4), 128), f32),
             vmem((6 * width, 512), bf16),
-            vmem((width * 8, 128), f32),
+            vmem((tile_y * spread_stride(8 * depth), 128), f32),
             vmem((3 * width, 512), bf16),
             vmem((3 * width, 512), bf16),
-            vmem((6 * 32 * tile_x, width), f32),
-            vmem((3 * 8 * tile_x, width), f32),
+            vmem((6 * 32 * spread_stride(tile_x), width), f32),
+            vmem((3 * 8 * spread_stride(tile_x), width), f32),
             vmem((24, tile_x, width), f32),
             vmem((24, tile_x, width), f32),
         ]

time: 64.7 us -> 61.1 us (0.944)
  Pallas kernels: 63.9 us -> 60.3 us
    pallas_call x1, Pallas kernels: 62.2 us -> 58.6 us  [per_device(): pl.pallas_call(functools.partial(step_kernel, (n_gx, n_gy), tile_x, tile_...]
where the time goes in v3:
time: 61.1 us; the launch traced here: 60.9 us
  Pallas kernels  60.3 us (99%)
  between operations  0.64 us (1%)
    pallas_call x1, Pallas kernels, per_device(): pl.pallas_call(functools.partial(step_kernel, (n_gx, n_gy), tile_x, tile_...  58.6 us
    pallas_call x1, Pallas kernels, per_device(): pl.pallas_call(functools.partial(format_kernel, depth), out_shape=(part,...  1.67 us

profile of v3, /device:TPU:0, one launch (start us, length us, event | category | flops | bytes accessed | tf_op | source)
XLA Modules:
  0.0 60.9 jit_solution(4620690672053061807)
XLA Ops:
  0.6 58.6 %step.1.value_ref = f32[12,16,128]{2,1,0:T(8,128)} custom-call(s32[2,16,4,32]{3,2,1,0:T(4,128)} %bitcast.3, bf16[64,512]{1,0:T(8,128)(2,1)} %constant.4.clone.square_ref, bf16[16,512]{1,0:T(8,128)(2,1)} %constant.5.clone.shape_ref, bf16[3,16,32,2048]{3,2,1,0:T(8,128)(2,1)} %grad_hbm.1, s32[16,32,2048]{2,1,0:T(8,128)} %mask_hbm.1, ...), custom_call_target="tpu_custom_call" | custom-call | tf_op jit(solution)/shard_map/step/pallas_call | solution.py:686
  59.2 1.7 %format.1 = (f32[3,5,16,32]{3,2,1,0:T(8,128)}, f32[3,5,16,32]{3,2,1,0:T(8,128)}) custom-call(f32[12,16,128]{2,1,0:T(8,128)} %step.1.value_ref), custom_call_target="tpu_custom_call" | custom-call | tf_op jit(solution)/shard_map/format/pallas_call | solution.py:744

commit v4 on v3

--- a/solution.py
+++ b/solution.py
@@ -70,9 +70,9 @@
     tile_x,
     tile_y,
     depth,
-    offset_ref,
-    square_ref,
-    shape_ref,
+    offset_hbm,
+    square_hbm,
+    shape_hbm,
     grad_hbm,
     mask_hbm,
     scan_ref,
@@ -113,6 +113,9 @@
     got_x,
     own_y,
     got_y,
+    offset_ref,
+    square_ref,
+    shape_ref,
     table_ref,
     source_ref,
     local_sems,
@@ -293,12 +296,14 @@
                 )
 
     lax.fori_loop(0, 2, start_first, 0)
-    extent = (tile_x, depth, tile_y)
-    pos_x, layers, pos_y = [lax.broadcasted_iota(jnp.int32, extent, k) for k in range(3)]
-    table = (pos_y + offset_ref[1] + BOUND) * stride_y
-    table_ref[...] = table + (layers * span_x + pos_x + offset_ref[0] + BOUND) * 4
-    table_copy = pltpu.make_async_copy(table_ref, source_ref, local_sems.at[5, 0])
-    table_copy.start()
+    small_copies = [
+        pltpu.make_async_copy(one, other, local_sems.at[5, k])
+        for k, (one, other) in enumerate(
+            ((square_hbm, square_ref), (offset_hbm, offset_ref), (shape_hbm, shape_ref))
+        )
+    ]
+    for one in small_copies:
+        one.start()
     pl.semaphore_wait(barrier, n_gx - 1 + n_gy - 1 + corners)
     begin(y_copies())
     for parts in (edges, rest):
@@ -333,6 +338,14 @@
                 hess_ref[rows, :] = value[first : first + 8]
         return carry
 
+    for one in small_copies:
+        one.wait()
+    extent = (tile_x, depth, tile_y)
+    pos_x, layers, pos_y = [lax.broadcasted_iota(jnp.int32, extent, k) for k in range(3)]
+    table = (pos_y + offset_ref[1] + BOUND) * stride_y
+    table_ref[...] = table + (layers * span_x + pos_x + offset_ref[0] + BOUND) * 4
+    table_copy = pltpu.make_async_copy(table_ref, source_ref, local_sems.at[5, 3])
+    table_copy.start()
     lax.fori_loop(0, tile_x, hessian_row, 0)
     table_copy.wait()
     arrive(y_copies())
@@ -374,16 +387,10 @@
         for one in second_copies(x):
             one.wait()
 
-        def fetch(block, inner_carry):
-            for inner in range(4):
-                y = block * 4 + inner
-                for layer in range(depth):
-                    row = source_ref[x, layer, y]
-                    rows = pl.ds(y * stride_f + layer * 8, 8)
-                    fetched_ref[rows, :] = wide_ref[pl.ds(row, 8), :]
-            return inner_carry
-
-        lax.fori_loop(0, tile_y // 4, fetch, 0)
+        for y in range(tile_y):
+            for layer in range(depth):
+                row = source_ref[x, layer, y]
+                fetched_ref[pl.ds(y * stride_f + layer * 8, 8), :] = wide_ref[pl.ds(row, 8), :]
         for layer in range(depth):
             for chunk in range(4):
                 lanes = pl.ds(layer * 512 + chunk * 128, 128)
@@ -685,8 +692,8 @@
     anywhere = pl.BlockSpec(memory_space=pl.ANY)
     packed = pl.pallas_call(
         functools.partial(step_kernel, (n_gx, n_gy), tile_x, tile_y, depth),
-        out_shape=jax.ShapeDtypeStruct((12, tile_x, width), f32),
-        in_specs=[whole] * 3 + [anywhere] * 5,
+        out_shape=vmem((12, tile_x, width), f32),
+        in_specs=[anywhere] * 8,
         out_specs=whole,
         scratch_shapes=[
             vmem((3, tile_x, tile_y, column), bf16),
@@ -717,6 +724,9 @@
             vmem((n_gx - 1, 8, width), f32),
             vmem((8, width), f32),
             vmem((n_gy - 1, 8, width), f32),
+            vmem((2, tile_x, depth, tile_y), jnp.int32),
+            vmem(square_table.shape, bf16),
+            vmem(shape_table.shape, bf16),
             vmem((tile_x, depth, tile_y), jnp.int32),
             pltpu.SMEM((tile_x, depth, tile_y), jnp.int32),
             dma((6, tile_x)),
@@ -746,6 +756,7 @@
         out_shape=(part, part),
         in_specs=[whole],
         out_specs=(whole, whole),
+        compiler_params=pltpu.CompilerParams(vmem_limit_bytes=2**21),
         name="format",
     )(packed)
 

time: 61.1 us -> 57.5 us (0.941)
  Pallas kernels: 60.3 us -> 56.8 us
    pallas_call x1, Pallas kernels: 58.6 us -> 56 us  [per_device(): pl.pallas_call(functools.partial(step_kernel, (n_gx, n_gy), tile_x, tile_...]
    pallas_call x1, Pallas kernels: 1.67 us -> 0.78 us  [per_device(): pl.pallas_call(functools.partial(format_kernel, depth), out_shape=(part,...]
where the time goes in v4:
time: 57.5 us; the launch traced here: 57.4 us
  Pallas kernels  56.8 us (99%)
  between operations  0.64 us (1%)
    pallas_call x1, Pallas kernels, per_device(): pl.pallas_call(functools.partial(step_kernel, (n_gx, n_gy), tile_x, tile_...  56 us

profile of v4, /device:TPU:0, one launch (start us, length us, event | category | flops | bytes accessed | tf_op | source)
XLA Modules:
  0.0 57.4 jit_solution(6012550560509403253)
XLA Ops:
  0.6 56.0 %step.1.value_ref = f32[12,16,128]{2,1,0:T(8,128)S(1)} custom-call(s32[2,16,4,32]{3,2,1,0:T(4,128)} %bitcast.3, bf16[64,512]{1,0:T(8,128)(2,1)} %constant.4.clone.square_hbm, bf16[16,512]{1,0:T(8,128)(2,1)} %constant.5.clone.shape_hbm, bf16[3,16,32,2048]{3,2,1,0:T(8,128)(2,1)} %grad_hbm.1, s32[16,32,2048]{2,1,0:T(8,128)} %mask_hbm.1, ...), custom_call_target="tpu_custom_call" | custom-call | tf_op jit(solution)/shard_map/step/pallas_call | solution.py:693
  56.6 0.8 %format.1 = (f32[3,5,16,32]{3,2,1,0:T(8,128)}, f32[3,5,16,32]{3,2,1,0:T(8,128)}) custom-call(f32[12,16,128]{2,1,0:T(8,128)S(1)} %step.1.value_ref), custom_call_target="tpu_custom_call" | custom-call | tf_op jit(solution)/shard_map/format/pallas_call | solution.py:754

commit v5 on v4

--- a/solution.py
+++ b/solution.py
@@ -62,7 +62,10 @@
 
 
 def row_of(turn, tile_x):
-    return jnp.where(turn < tile_x - BOUND, turn + BOUND, tile_x - 1 - turn)
+    place = turn - (tile_x - 2 * BOUND - 1)
+    upper = tile_x - BOUND - 1 + place // 2
+    edge = jnp.where(place % 2 == 0, upper, BOUND - 1 - place // 2)
+    return jnp.where(place < 0, turn + BOUND, edge)
 
 
 def step_kernel(
@@ -270,11 +273,24 @@
             one.start()
         return carry
 
-    for buffer in (in_w, in_e, in_s, in_n, in_sw, in_ne, in_nw, in_se):
-        buffer[...] = jnp.zeros_like(buffer)
-    for buffer in (out_e, out_w, out_n, out_s):
-        buffer[...] = jnp.zeros_like(buffer)
     barrier = pltpu.get_barrier_semaphore()
+    there_x = {-1: not_first_x, 0: gx >= 0, 1: not_last_x}
+    there_y = {-1: not_first_y, 0: gy >= 0, 1: not_last_y}
+
+    def greet(target, steps):
+        found = 0
+        for dx, dy in steps:
+            present = both(there_x[dx], there_y[dy])
+            found = found + jnp.where(present, 1, 0)
+
+            @pl.when(present)
+            def _(dx=dx, dy=dy):
+                pl.semaphore_signal(
+                    target, inc=1, device_id=(gx + dx, gy + dy), device_id_type=MESH
+                )
+
+        return found
+
     for k in range(1, n_gx):
         pl.semaphore_signal(
             barrier, inc=1, device_id=((gx + k) % n_gx, gy), device_id_type=MESH
@@ -283,18 +299,7 @@
         pl.semaphore_signal(
             barrier, inc=1, device_id=(gx, (gy + k) % n_gy), device_id_type=MESH
         )
-    corners = 0
-    for dx, there_x in ((-1, not_first_x), (1, not_last_x)):
-        for dy, there_y in ((-1, not_first_y), (1, not_last_y)):
-            present = both(there_x, there_y)
-            corners = corners + jnp.where(present, 1, 0)
-
-            @pl.when(present)
-            def _(dx=dx, dy=dy):
-                pl.semaphore_signal(
-                    barrier, inc=1, device_id=(gx + dx, gy + dy), device_id_type=MESH
-                )
-
+    corners = greet(barrier, [(dx, dy) for dx in (-1, 1) for dy in (-1, 1)])
     lax.fori_loop(0, 2, start_first, 0)
     small_copies = [
         pltpu.make_async_copy(one, other, local_sems.at[5, k])
@@ -309,10 +314,27 @@
     for parts in (edges, rest):
         for k in range(BOUND + 1):
             begin(after_parts(k, parts))
-        for k in range(BOUND):
-            begin(before_parts(BOUND - 1 - k, parts))
+            if k < BOUND:
+                begin(before_parts(BOUND - 1 - k, parts))
     lax.fori_loop(2, tile_x, start_first, 0)
     lax.fori_loop(0, tile_x, start_second, 0)
+    for buffer, dx, dy in (
+        (in_w, -1, 0),
+        (in_e, 1, 0),
+        (in_s, 0, -1),
+        (in_n, 0, 1),
+        (in_sw, -1, -1),
+        (in_ne, 1, 1),
+        (in_nw, -1, 1),
+        (in_se, 1, -1),
+    ):
+
+        @pl.when(jnp.logical_not(both(there_x[dx], there_y[dy])))
+        def _(buffer=buffer):
+            buffer[...] = jnp.zeros_like(buffer)
+
+    for buffer in (out_e, out_w, out_n, out_s):
+        buffer[...] = jnp.zeros_like(buffer)
 
     def hessian_row(x, carry):
         for one in first_copies(x):
@@ -356,7 +378,6 @@
 
     lax.fori_loop(0, tile_x, convert, 0)
     head = tile_x - 2 * BOUND - 1
-    turned = tile_x - BOUND
 
     def load_row(turn, carry):
         @pl.when(both(turn >= head - BOUND - 1, turn < head))
@@ -371,15 +392,17 @@
             arrive(before_parts(k, edges))
             begin(before_corners(k))
 
-        @pl.when(both(turn >= head, turn < turned))
+        place = turn - head
+
+        @pl.when(both(place >= 0, place % 2 == 0))
         def _():
-            k = turn - head
+            k = place // 2
             arrive(after_parts(k, rest) + after_corners(k))
             put_band(after_ref, k, BOUND + tile_x + k, not_last_x)
 
-        @pl.when(turn >= turned)
+        @pl.when(both(place >= 0, place % 2 == 1))
         def _():
-            k = tile_x - 1 - turn
+            k = BOUND - 1 - place // 2
             arrive(before_parts(k, rest) + before_corners(k))
             put_band(before_ref, k, k, not_first_x)
 
@@ -439,18 +462,18 @@
 
     def copies(phase):
         table = [
+            (out_e, lower, in_sw, 1, 1),
             (out_e, None, in_w, 1, 0),
             (out_n, None, in_s, 0, 1),
-            (out_e, lower, in_sw, 1, 1),
-            (out_w, None, in_e, -1, 0),
-            (out_s, None, in_n, 0, -1),
             (out_w, upper, in_ne, -1, -1),
             (out_e, upper, in_nw, 1, -1),
             (out_w, lower, in_se, -1, 1),
+            (out_w, None, in_e, -1, 0),
+            (out_s, None, in_n, 0, -1),
         ]
         if phase == PHASES - 1:
             table = table[:3]
-        found = []
+        far, near = ([], [])
         for k, (src, rows, dst, dx, dy) in enumerate(table):
             send_ok, recv_ok = (gx >= 0, gx >= 0)
             if dx:
@@ -467,8 +490,8 @@
                 recv_sems.at[phase, k],
                 (gx + dx, gy + dy),
             )
-            found.append((one, send_ok, recv_ok))
-        return found
+            (far if dx else near).append((one, send_ok, recv_ok))
+        return (far, near)
 
     def assemble(phase, partial, meanwhile):
         folded = {}
@@ -482,41 +505,47 @@
                     folded[i, j, 3 + c] = jnp.where(topmost, over, 0.0)
                 for c in range(3):
                     folded[i, j, c] = found[c]
-        total, right = ([], [])
-        north = jnp.zeros((tile_x, width), jnp.float32)
-        south = jnp.zeros((tile_x, width), jnp.float32)
+        total, right, edge_x, edge_c = ([], [], [], [])
         for a in range(6):
             kept = [
                 folded[i, 0, a] + jnp.where(first_y, 0.0, roll(folded[i, 1, a], 1, 1))
                 for i in range(2)
             ]
-            mine = kept[0] + shift_x(kept[1])
-            side = folded[0, 1, a] + shift_x(folded[1, 1, a])
-            edge_x = kept[1][tile_x - 1 :]
-            edge_c = folded[1, 1, a][tile_x - 1 :]
-            out_e[phase, a : a + 1, :] = edge_x
-            out_e[phase, 8 + a : 9 + a, :] = edge_c
-            out_w[phase, a : a + 1, :] = mine[0:1]
-            out_w[phase, 8 + a : 9 + a, :] = side[0:1]
-            out_n[phase, tile_x + a : tile_x + a + 1, :] = edge_c
-            out_s[phase, tile_x + a : tile_x + a + 1, :] = edge_x
-            north = jnp.where(in_tile == a, roll(side, a + 1, 1), north)
-            south = jnp.where(in_tile == a, roll(mine, a, 1), south)
-            total.append(mine)
-            right.append(side)
+            total.append(kept[0] + shift_x(kept[1]))
+            right.append(folded[0, 1, a] + shift_x(folded[1, 1, a]))
+            edge_x.append(kept[1][tile_x - 1 :])
+            edge_c.append(folded[1, 1, a][tile_x - 1 :])
+            out_e[phase, a : a + 1, :] = edge_x[a]
+            out_e[phase, 8 + a : 9 + a, :] = edge_c[a]
+            out_w[phase, a : a + 1, :] = total[a][0:1]
+            out_w[phase, 8 + a : 9 + a, :] = right[a][0:1]
+        far, near = copies(phase)
+        begin(far)
+        north = jnp.zeros((tile_x, width), jnp.float32)
+        south = jnp.zeros((tile_x, width), jnp.float32)
+        for a in range(6):
+            north = jnp.where(in_tile == a, roll(right[a], a + 1, 1), north)
+            south = jnp.where(in_tile == a, roll(total[a], a, 1), south)
+            out_n[phase, tile_x + a : tile_x + a + 1, :] = edge_c[a]
+            out_s[phase, tile_x + a : tile_x + a + 1, :] = edge_x[a]
         out_n[phase, body, :] = north
         out_s[phase, body, :] = south
-        begin(copies(phase))
+        begin(near)
         meanwhile()
-        arrive(copies(phase))
+        arrive(near)
+        from_s = in_s[phase, body, :]
+        whole = [
+            total[a] + jnp.where(first_y, roll(from_s, -(tile_y + a), 1), 0.0) for a in range(6)
+        ]
+        if phase < PHASES - 1:
+            from_n = in_n[phase, body, :]
+            right = [right[a] + roll(from_n, turn_y - a, 1) for a in range(6)]
+        arrive(far)
         line = in_w[phase, upper, :] + jnp.where(
             first_8, roll(in_sw[phase], -turn_y, 1), 0.0
         )
-        from_s = in_s[phase, body, :]
         whole = [
-            total[a]
-            + jnp.where(first_x, line[a : a + 1], 0.0)
-            + jnp.where(first_y, roll(from_s, -(tile_y + a), 1), 0.0)
+            whole[a] + jnp.where(first_x, line[a : a + 1], 0.0)
             for a in range(6)
         ]
         if phase == PHASES - 1:
@@ -529,10 +558,8 @@
         corner = out_e[phase, lower, :] + in_e[phase, lower, :] + roll(corner, turn_y, 1)
         corner = jnp.where(both(not_last_x, not_last_y), corner, 0.0)
         corner = jnp.where(last_8, corner, roll(side_x, -1, 1))
-        from_n = in_n[phase, body, :]
         for a in range(6):
             side = right[a] + jnp.where(first_x, line[a : a + 1], 0.0)
-            side = side + roll(from_n, turn_y - a, 1)
             side = jnp.where(not_last_y, side, 0.0)
             next_x = jnp.where(last_x, side_x[a : a + 1], roll(whole[a], -1, 0))
             next_y = jnp.where(last_y, side, roll(whole[a], -1, 1))
@@ -655,7 +682,8 @@
         out_ref[a] = inc
         out_ref[6 + a] = res
     for phase in range(PHASES):
-        sent(copies(phase))
+        for group in copies(phase):
+            sent(group)
     for one in along_x() + along_y():
         one.wait_send()
     sent(y_copies())

time: 57.5 us -> 55.9 us (0.972)
  Pallas kernels: 56.8 us -> 55.1 us
    pallas_call x1, Pallas kernels: 56 us -> 54.4 us  [per_device(): pl.pallas_call(functools.partial(step_kernel, (n_gx, n_gy), tile_x, tile_...]
where the time goes in v5:
time: 55.9 us; the launch traced here: 55.8 us
  Pallas kernels  55.1 us (99%)
  between operations  0.64 us (1%)
    pallas_call x1, Pallas kernels, per_device(): pl.pallas_call(functools.partial(step_kernel, (n_gx, n_gy), tile_x, tile_...  54.4 us

profile of v5, /device:TPU:0, one launch (start us, length us, event | category | flops | bytes accessed | tf_op | source)
XLA Modules:
  0.0 55.8 jit_solution(18375200615358462490)
XLA Ops:
  0.6 54.4 %step.1.value_ref = f32[12,16,128]{2,1,0:T(8,128)S(1)} custom-call(s32[2,16,4,32]{3,2,1,0:T(4,128)} %bitcast.3, bf16[64,512]{1,0:T(8,128)(2,1)} %constant.4.clone.square_hbm, bf16[16,512]{1,0:T(8,128)(2,1)} %constant.5.clone.shape_hbm, bf16[3,16,32,2048]{3,2,1,0:T(8,128)(2,1)} %grad_hbm.1, s32[16,32,2048]{2,1,0:T(8,128)} %mask_hbm.1, ...), custom_call_target="tpu_custom_call" | custom-call | tf_op jit(solution)/shard_map/step/pallas_call | solution.py:721
  55.0 0.8 %format.1 = (f32[3,5,16,32]{3,2,1,0:T(8,128)}, f32[3,5,16,32]{3,2,1,0:T(8,128)}) custom-call(f32[12,16,128]{2,1,0:T(8,128)S(1)} %step.1.value_ref), custom_call_target="tpu_custom_call" | custom-call | tf_op jit(solution)/shard_map/format/pallas_call | solution.py:782

commit v6 on v5

--- a/solution.py
+++ b/solution.py
@@ -114,8 +114,6 @@
     in_se,
     own_x,
     got_x,
-    own_y,
-    got_y,
     offset_ref,
     square_ref,
     shape_ref,
@@ -128,8 +126,6 @@
     recv_sems,
     send_x,
     recv_x,
-    send_y,
-    recv_y,
 ):
     n_gx, n_gy = sizes
     gx = lax.axis_index("gx")
@@ -277,29 +273,14 @@
     there_x = {-1: not_first_x, 0: gx >= 0, 1: not_last_x}
     there_y = {-1: not_first_y, 0: gy >= 0, 1: not_last_y}
 
-    def greet(target, steps):
-        found = 0
-        for dx, dy in steps:
-            present = both(there_x[dx], there_y[dy])
-            found = found + jnp.where(present, 1, 0)
-
-            @pl.when(present)
-            def _(dx=dx, dy=dy):
-                pl.semaphore_signal(
-                    target, inc=1, device_id=(gx + dx, gy + dy), device_id_type=MESH
-                )
-
-        return found
-
-    for k in range(1, n_gx):
+    for k in range(1, n_gx * n_gy):
+        other = (gx * n_gy + gy + k) % (n_gx * n_gy)
         pl.semaphore_signal(
-            barrier, inc=1, device_id=((gx + k) % n_gx, gy), device_id_type=MESH
+            barrier,
+            inc=1,
+            device_id=(other // n_gy, other % n_gy),
+            device_id_type=MESH,
         )
-    for k in range(1, n_gy):
-        pl.semaphore_signal(
-            barrier, inc=1, device_id=(gx, (gy + k) % n_gy), device_id_type=MESH
-        )
-    corners = greet(barrier, [(dx, dy) for dx in (-1, 1) for dy in (-1, 1)])
     lax.fori_loop(0, 2, start_first, 0)
     small_copies = [
         pltpu.make_async_copy(one, other, local_sems.at[5, k])
@@ -309,7 +290,7 @@
     ]
     for one in small_copies:
         one.start()
-    pl.semaphore_wait(barrier, n_gx - 1 + n_gy - 1 + corners)
+    pl.semaphore_wait(barrier, n_gx * n_gy - 1)
     begin(y_copies())
     for parts in (edges, rest):
         for k in range(BOUND + 1):
@@ -588,23 +569,21 @@
                             total = term if total is None else total + term
                     value_ref[3 * n + c, rows, :] = total
 
-    def exchange(own, got, sends, receives, index, count, target):
-        return [
-            remote(
-                own,
-                got.at[k - 1],
-                sends.at[k - 1],
-                receives.at[k - 1],
-                target((index + k) % count),
+    def everyone():
+        place = gx * n_gy + gy
+        found = []
+        for k in range(1, n_gx * n_gy):
+            other = (place + k) % (n_gx * n_gy)
+            found.append(
+                remote(
+                    own_x,
+                    got_x.at[k - 1],
+                    send_x.at[k - 1],
+                    recv_x.at[k - 1],
+                    (other // n_gy, other % n_gy),
+                )
             )
-            for k in range(1, count)
-        ]
-
-    def along_x():
-        return exchange(own_x, got_x, send_x, recv_x, gx, n_gx, lambda t: (t, gy))
-
-    def along_y():
-        return exchange(own_y, got_y, send_y, recv_y, gy, n_gy, lambda t: (gx, t))
+        return found
 
     def gather(found, own, got, count):
         for one in found:
@@ -644,21 +623,17 @@
         inner(base[2], base[2]),
         last,
     ]
+    spot = lane[0:1]
+    packed = jnp.zeros((1, width), jnp.float32)
     for k in range(6):
-        own_x[k : k + 1, :] = rows[k]
-    own_x[6:8, :] = jnp.zeros((2, width), jnp.float32)
-    for one in along_x():
+        packed = jnp.where(spot == k, jnp.sum(rows[k], axis=1, keepdims=True), packed)
+    own_x[...] = packed
+    for one in everyone():
         one.start()
 
-    def pass_on():
-        own_y[...] = gather(along_x(), own_x, got_x, n_gx)
-        for one in along_y():
-            one.start()
-
-    base.append(assemble(ITERS, value_part, pass_on))
-    sums = gather(along_y(), own_y, got_y, n_gy)
-    sums = jnp.sum(sums, axis=1, keepdims=True)
-    h = [sums[k : k + 1] for k in range(6)]
+    base.append(assemble(ITERS, value_part, nothing))
+    sums = gather(everyone(), own_x, got_x, n_gx * n_gy)
+    h = [sums[:, k : k + 1] for k in range(6)]
     sigma = tikhonov / UNIT
     a0 = h[1] / h[0]
     n1 = h[2] - a0 * h[1]
@@ -684,7 +659,7 @@
     for phase in range(PHASES):
         for group in copies(phase):
             sent(group)
-    for one in along_x() + along_y():
+    for one in everyone():
         one.wait_send()
     sent(y_copies())
     for k in range(BOUND + 1):
@@ -748,10 +723,8 @@
             for rows in (16, 16, tile_x + 8, tile_x + 8) * 2 + (8, 8, 8, 8)
         ]
         + [
-            vmem((8, width), f32),
-            vmem((n_gx - 1, 8, width), f32),
-            vmem((8, width), f32),
-            vmem((n_gy - 1, 8, width), f32),
+            vmem((1, width), f32),
+            vmem((n_gx * n_gy - 1, 1, width), f32),
             vmem((2, tile_x, depth, tile_y), jnp.int32),
             vmem(square_table.shape, bf16),
             vmem(shape_table.shape, bf16),
@@ -762,10 +735,8 @@
             dma((halos,)),
             dma((PHASES, 8)),
             dma((PHASES, 8)),
-            dma((n_gx - 1,)),
-            dma((n_gx - 1,)),
-            dma((n_gy - 1,)),
-            dma((n_gy - 1,)),
+            dma((n_gx * n_gy - 1,)),
+            dma((n_gx * n_gy - 1,)),
         ],
         compiler_params=pltpu.CompilerParams(collective_id=0, has_side_effects=True),
         name="step",

time: 55.9 us -> 55.3 us (0.989)
  Pallas kernels: 55.1 us -> 54.5 us
    pallas_call x1, Pallas kernels: 54.4 us -> 53.7 us  [per_device(): pl.pallas_call(functools.partial(step_kernel, (n_gx, n_gy), tile_x, tile_...]
where the time goes in v6:
time: 55.3 us; the launch traced here: 55.1 us
  Pallas kernels  54.5 us (99%)
  between operations  0.64 us (1%)
    pallas_call x1, Pallas kernels, per_device(): pl.pallas_call(functools.partial(step_kernel, (n_gx, n_gy), tile_x, tile_...  53.7 us

profile of v6, /device:TPU:0, one launch (start us, length us, event | category | flops | bytes accessed | tf_op | source)
XLA Modules:
  0.0 55.1 jit_solution(15880514863058894946)
XLA Ops:
  0.6 53.7 %step.1.value_ref = f32[12,16,128]{2,1,0:T(8,128)S(1)} custom-call(s32[2,16,4,32]{3,2,1,0:T(4,128)} %bitcast.3, bf16[64,512]{1,0:T(8,128)(2,1)} %constant.4.clone.square_hbm, bf16[16,512]{1,0:T(8,128)(2,1)} %constant.5.clone.shape_hbm, bf16[3,16,32,2048]{3,2,1,0:T(8,128)(2,1)} %grad_hbm.1, s32[16,32,2048]{2,1,0:T(8,128)} %mask_hbm.1, ...), custom_call_target="tpu_custom_call" | custom-call | tf_op jit(solution)/shard_map/step/pallas_call | solution.py:696
  54.4 0.8 %format.1 = (f32[3,5,16,32]{3,2,1,0:T(8,128)}, f32[3,5,16,32]{3,2,1,0:T(8,128)}) custom-call(f32[12,16,128]{2,1,0:T(8,128)S(1)} %step.1.value_ref), custom_call_target="tpu_custom_call" | custom-call | tf_op jit(solution)/shard_map/format/pallas_call | solution.py:753

commit v7 on v6

--- a/solution.py
+++ b/solution.py
@@ -708,13 +708,13 @@
             vmem((BOUND + 1, tile_y, column), bf16),
             vmem((span_x, EDGE, column), bf16),
             vmem((span_x, EDGE, column), bf16),
-            vmem((span_y * spread_stride(depth * span_x * 4), 128), f32),
+            vmem(((span_y + 1) * spread_stride(depth * span_x * 4), 128), f32),
             vmem((6 * width, 512), bf16),
-            vmem((tile_y * spread_stride(8 * depth), 128), f32),
+            vmem(((tile_y + 1) * spread_stride(8 * depth), 128), f32),
             vmem((3 * width, 512), bf16),
             vmem((3 * width, 512), bf16),
-            vmem((6 * 32 * spread_stride(tile_x), width), f32),
-            vmem((3 * 8 * spread_stride(tile_x), width), f32),
+            vmem(((6 * 32 + 1) * spread_stride(tile_x), width), f32),
+            vmem(((3 * 8 + 1) * spread_stride(tile_x), width), f32),
             vmem((24, tile_x, width), f32),
             vmem((24, tile_x, width), f32),
         ]

time: 55.3 us -> 55.3 us (level)
  no operation moved by 1% of the time
where the time goes in v7:
time: 55.3 us; the launch traced here: 55.1 us
  Pallas kernels  54.5 us (99%)
  between operations  0.64 us (1%)
    pallas_call x1, Pallas kernels, per_device(): pl.pallas_call(functools.partial(step_kernel, (n_gx, n_gy), tile_x, tile_...  53.7 us

profile of v7, /device:TPU:0, one launch (start us, length us, event | category | flops | bytes accessed | tf_op | source)
XLA Modules:
  0.0 55.1 jit_solution(17738315732921934679)
XLA Ops:
  0.6 53.7 %step.1.value_ref = f32[12,16,128]{2,1,0:T(8,128)S(1)} custom-call(s32[2,16,4,32]{3,2,1,0:T(4,128)} %bitcast.3, bf16[64,512]{1,0:T(8,128)(2,1)} %constant.4.clone.square_hbm, bf16[16,512]{1,0:T(8,128)(2,1)} %constant.5.clone.shape_hbm, bf16[3,16,32,2048]{3,2,1,0:T(8,128)(2,1)} %grad_hbm.1, s32[16,32,2048]{2,1,0:T(8,128)} %mask_hbm.1, ...), custom_call_target="tpu_custom_call" | custom-call | tf_op jit(solution)/shard_map/step/pallas_call | solution.py:696
  54.4 0.8 %format.1 = (f32[3,5,16,32]{3,2,1,0:T(8,128)}, f32[3,5,16,32]{3,2,1,0:T(8,128)}) custom-call(f32[12,16,128]{2,1,0:T(8,128)S(1)} %step.1.value_ref), custom_call_target="tpu_custom_call" | custom-call | tf_op jit(solution)/shard_map/format/pallas_call | solution.py:753

commit v8 on v7

--- a/solution.py
+++ b/solution.py
@@ -572,8 +572,9 @@
     def everyone():
         place = gx * n_gy + gy
         found = []
-        for k in range(1, n_gx * n_gy):
-            other = (place + k) % (n_gx * n_gy)
+        count = n_gx * n_gy
+        for k in sorted(range(1, count), key=lambda k: min(k, count - k)):
+            other = (place + k) % count
             found.append(
                 remote(
                     own_x,

time: 55.3 us -> 55.3 us (level)
  no operation moved by 1% of the time
where the time goes in v8:
time: 55.3 us; the launch traced here: 55.2 us
  Pallas kernels  54.5 us (99%)
  between operations  0.64 us (1%)
    pallas_call x1, Pallas kernels, per_device(): pl.pallas_call(functools.partial(step_kernel, (n_gx, n_gy), tile_x, tile_...  53.7 us

profile of v8, /device:TPU:0, one launch (start us, length us, event | category | flops | bytes accessed | tf_op | source)
XLA Modules:
  0.0 55.2 jit_solution(17141415219797748564)
XLA Ops:
  0.6 53.7 %step.1.value_ref = f32[12,16,128]{2,1,0:T(8,128)S(1)} custom-call(s32[2,16,4,32]{3,2,1,0:T(4,128)} %bitcast.3, bf16[64,512]{1,0:T(8,128)(2,1)} %constant.4.clone.square_hbm, bf16[16,512]{1,0:T(8,128)(2,1)} %constant.5.clone.shape_hbm, bf16[3,16,32,2048]{3,2,1,0:T(8,128)(2,1)} %grad_hbm.1, s32[16,32,2048]{2,1,0:T(8,128)} %mask_hbm.1, ...), custom_call_target="tpu_custom_call" | custom-call | tf_op jit(solution)/shard_map/step/pallas_call | solution.py:697
  54.4 0.8 %format.1 = (f32[3,5,16,32]{3,2,1,0:T(8,128)}, f32[3,5,16,32]{3,2,1,0:T(8,128)}) custom-call(f32[12,16,128]{2,1,0:T(8,128)S(1)} %step.1.value_ref), custom_call_target="tpu_custom_call" | custom-call | tf_op jit(solution)/shard_map/format/pallas_call | solution.py:754
